TPU v7x, 256 devices: a whole 4x4x8 slice. The times are simulated.
256 devices in a mesh: slab: 4 (over x), energy: 64 (over y, z, core).
Axes of the slice: x: 4, y: 4, z: 8, core: 2. Of those that a mesh axis runs over, the one named last changes fastest.
Arguments:
- energies: float32 [64], P('energy'), may hold values from -1 to 1
- broadening: float32 [64], P('energy'), may hold values from 0.3 to 1
- hamiltonian: float32 [1024, 256], P('slab'), as said below
- coupling: float32 [1024, 256], P('slab'), may hold values from -0.21875 to 0.21875
- propagator: float32 [2, 6, 64, 64], replicated, may hold values from -0.75 to 0.75
- neighbors: int32 [1024, 32], P('slab'), may hold values from 0 to 255, as said below
- phonon_modes: int32 [1024, 32], P('slab'), may hold values from 0 to 5
Outputs:
- green_blocks: float32 [64, 2, 1024, 256], P('energy', None, 'slab')
- self_energy: float32 [64, 2, 32768], P('energy', None, 'slab')
Inputs may be any that keep to these rules, and one draw needn't show every extreme that they name: `hamiltonian`: each block of 256 rows is symmetric. `neighbors`: an orbital is never its own neighbour.
All inputs are finite; a program needn't handle non-finite values.
Results may differ from a plain program's by a relative error of at most 0.0001.
Values sent between devices are 32-bit elements; how exact they have to be, the bound alone decides.
No kernel may reach another device: no remote copies, remote signals or barrier semaphores. Data moves between devices by JAX's collectives and lax.ppermute only.
A program may use at most 128 MiB of HBM per device.

v0:
```python
import math

import jax
import jax.numpy as jnp
from jax import lax
from jax.sharding import Mesh
from jax.sharding import PartitionSpec as P

B = 256
NEIGH = 32
ENERGY = ("energy_0", "energy_1", "energy_2")


HIGHEST = lax.Precision.HIGHEST


def shifted_2(block, axis, distance):
    devices = range(lax.axis_size(axis))
    route = [(i - distance, i) for i in devices if i - distance in devices]
    return lax.ppermute(block, axis, route)


def in_blocks(x, dim, count):
    before, after = (x.shape[:dim], x.shape[dim + 1 :])
    return jnp.moveaxis(x.reshape(*before, count, -1, *after), dim, 0)


def joined_along(parts, dim):
    parts = jnp.moveaxis(parts, 0, dim)
    lengths = parts.shape
    return parts.reshape(*lengths[:dim], lengths[dim] * lengths[dim + 1], *lengths[dim + 2 :])


def exchange_in_order(parts, axes, turns):
    inside = parts.shape[1:]
    whole = parts.reshape(*(lax.axis_size(a) for a in axes), *inside)
    for k in turns:
        whole = lax.all_to_all(whole, axes[k], k, k, tiled=True)
    return whole.reshape(-1, *inside)


def two_step_exchange(x, groups, turns, split_dim, concat_dim):
    count = lax.axis_size(groups[0]) * lax.axis_size(groups[1])
    parts = in_blocks(x, split_dim, count)
    return joined_along(exchange_in_order(parts, groups, turns), concat_dim)


def complex_product(left, right):
    left_real, left_imag = (left[:, 0], left[:, 1])
    right_real, right_imag = (right[:, 0], right[:, 1])
    first = jnp.matmul(left_real, right_real, precision=HIGHEST)
    second = jnp.matmul(left_imag, right_imag, precision=HIGHEST)
    mixed = jnp.matmul(left_real + left_imag, right_real + right_imag, precision=HIGHEST)
    return jnp.stack([first - second, mixed - first - second], axis=1)


def newton_step(schur, inverse):
    identity = jnp.eye(schur.shape[-1], dtype=jnp.float32)
    residue = -complex_product(schur, inverse)
    residue = residue.at[:, 0].add(2.0 * identity)
    return complex_product(inverse, residue)


def jacobi_refine(schur):
    identity = jnp.eye(schur.shape[-1], dtype=jnp.float32)
    diagonal = jnp.diagonal(schur, axis1=2, axis2=3)
    diag_real, diag_imag = (diagonal[:, 0], diagonal[:, 1])
    modulus = diag_real * diag_real + diag_imag * diag_imag
    inv_real = diag_real / modulus
    inv_imag = -diag_imag / modulus
    outer_real = (
        inv_real[:, :, None] * inv_real[:, None, :] - inv_imag[:, :, None] * inv_imag[:, None, :]
    )
    outer_imag = (
        inv_real[:, :, None] * inv_imag[:, None, :] + inv_imag[:, :, None] * inv_real[:, None, :]
    )
    schur_real, schur_imag = (schur[:, 0], schur[:, 1])
    first_real = 2.0 * identity * inv_real[:, :, None] - (
        outer_real * schur_real - outer_imag * schur_imag
    )
    first_imag = 2.0 * identity * inv_imag[:, :, None] - (
        outer_real * schur_imag + outer_imag * schur_real
    )
    first_iterate = jnp.stack([first_real, first_imag], axis=1)
    return newton_step(schur, first_iterate)


def convolve_modes(kernel, values, one_hot):
    spread = one_hot[:, None, None, :] * values[None]
    real_part = jnp.einsum(
        "mef,mfp->ep", kernel[0], spread[:, :, 0], precision=HIGHEST
    ) - jnp.einsum("mef,mfp->ep", kernel[1], spread[:, :, 1], precision=HIGHEST)
    imag_part = jnp.einsum(
        "mef,mfp->ep", kernel[0], spread[:, :, 1], precision=HIGHEST
    ) + jnp.einsum("mef,mfp->ep", kernel[1], spread[:, :, 0], precision=HIGHEST)
    return jnp.stack([real_part, imag_part], axis=1)


def body(energies, broadening, hamiltonian, coupling, propagator, neighbors, phonon_modes):
    coupling_scale = 2.0 * math.sqrt(B / NEIGH)
    e_dev = energies.shape[0]
    orbitals = hamiltonian.shape[0]
    listed = neighbors.shape[1]
    mode_count = propagator.shape[1]
    identity = jnp.eye(orbitals, dtype=jnp.float32)
    shifted = jnp.stack(
        [
            energies[:, None, None] * identity - hamiltonian[None],
            broadening[:, None, None] * identity,
        ],
        axis=1,
    )

    def advance(operand):
        through = jnp.matmul(
            jnp.matmul(coupling, operand[0], precision=HIGHEST), coupling.T, precision=HIGHEST
        )
        schur_new = shifted - through
        return (schur_new, jacobi_refine(schur_new))

    def remain(operand):
        return (operand[1], operand[2])

    slab_count = lax.axis_size("slab")
    slab_index = lax.axis_index("slab")
    incoming = jnp.zeros((e_dev, 2, orbitals, orbitals), jnp.float32)
    schur = jnp.zeros_like(incoming)
    inverse = jnp.zeros_like(incoming)
    for step_index in range(slab_count):
        schur, inverse = lax.cond(
            slab_index == step_index, advance, remain, (incoming, schur, inverse)
        )
        if step_index + 1 < slab_count:
            incoming = shifted_2(inverse, "slab", 1)
    pair_mask = (
        neighbors[:, :, None] == jnp.arange(orbitals, dtype=jnp.int32)[None, None, :]
    ).astype(jnp.float32)
    pair_green = jnp.einsum("ecij,ikj->ecik", inverse, pair_mask, precision=HIGHEST).reshape(
        e_dev, 2, orbitals * listed
    )
    modes_flat = phonon_modes.reshape(-1)
    mode_ids = jnp.arange(mode_count, dtype=jnp.int32)
    regrouped = two_step_exchange(pair_green, (("energy_0", "energy_1"), "energy_2"), (1, 0), 2, 0)
    local_pairs = regrouped.shape[2]
    local_modes = lax.dynamic_slice_in_dim(
        modes_flat, lax.axis_index(ENERGY) * local_pairs, local_pairs
    )
    one_hot = (local_modes[None, :] == mode_ids[:, None]).astype(jnp.float32)
    owned = coupling_scale * convolve_modes(propagator, regrouped, one_hot)
    self_part = lax.all_to_all(owned, ENERGY, split_axis=0, concat_axis=2, tiled=True)
    reshaped = self_part.reshape(e_dev, 2, orbitals, listed)
    self_dense = jnp.einsum("ecik,ikj->ecij", reshaped, pair_mask, precision=HIGHEST)
    residue = -complex_product(schur - self_dense, inverse)
    residue = residue.at[:, 0].add(2.0 * identity)
    green_block = complex_product(inverse, residue)
    return (green_block, self_part)


def solution(mesh):
    finer = Mesh(
        mesh.devices.reshape(mesh.shape["slab"], 4, 8, 2),
        ("slab", "energy_0", "energy_1", "energy_2"),
    )
    in_specs = (
        P(ENERGY),
        P(ENERGY),
        P("slab", None),
        P("slab", None),
        P(),
        P("slab", None),
        P("slab", None),
    )
    out_specs = (P(ENERGY, None, "slab", None), P(ENERGY, None, "slab"))
    return jax.shard_map(body, mesh=finer, in_specs=in_specs, out_specs=out_specs, check_vma=False)
```

profile of v0, /device:TPU:7, one launch (start us, length us, event | category | flops | bytes accessed | tf_op | source)
XLA Modules:
  0.0 228.3 jit_solution(10430764625841848425)
XLA Ops:
  2.0 1.0 subtract_bitcast_fusion.9
  3.0 0.9 conditional.4
  3.0 0.8 broadcast.3782
  3.9 1.3 collective-permute-start
  5.2 13.4 %collective-permute-done = f32[1,2,256,256]{3,2,1,0:T(8,128)S(1)} collective-permute-done((f32[1,2,256,256]{3,2,1,0:T(8,128)S(1)}, f32[1,2,256,256]{3,2,1,0:T(8,128)S(1)}, u32[]{:S(2)}, u32[]{:S(2)}) %collective-permute-start) | collective-permute-done | bytes 524320 | tf_op jit(solution)/shard_map/ppermute | solution.py:20
  18.6 0.0 copy-start.1
  18.6 0.0 copy-start.2
  18.6 1.4 collective-permute-start.1
  20.0 12.5 %collective-permute-done.1 = f32[1,2,256,256]{3,2,1,0:T(8,128)S(1)} collective-permute-done((f32[1,2,256,256]{3,2,1,0:T(8,128)S(1)}, f32[1,2,256,256]{3,2,1,0:T(8,128)S(1)}, u32[]{:S(2)}, u32[]{:S(2)}) %collective-permute-start.1) | collective-permute-done | bytes 524320 | tf_op jit(solution)/shard_map/ppermute | solution.py:20
  32.5 0.0 copy-start
  32.5 1.4 collective-permute-start.2
  34.0 0.0 copy-done.1
  34.0 0.1 copy.49
  34.1 0.0 copy-done.2
  34.1 0.1 copy.50
  34.2 0.1 reshape.5973
  34.3 0.1 dynamic_slice.3
  34.4 91.7 %collective-permute-done.2 = f32[1,2,256,256]{3,2,1,0:T(8,128)S(1)} collective-permute-done((f32[1,2,256,256]{3,2,1,0:T(8,128)S(1)}, f32[1,2,256,256]{3,2,1,0:T(8,128)S(1)}, u32[]{:S(2)}, u32[]{:S(2)}) %collective-permute-start.2) | collective-permute-done | bytes 524320 | tf_op jit(solution)/shard_map/ppermute | solution.py:20
  126.1 34.8 %conditional.7 = (f32[1,2,256,256]{3,2,1,0:T(8,128)}, f32[1,1,256,256]{3,2,1,0:T(8,128)}, f32[1,1,256,256]{3,2,1,0:T(8,128)}, f32[256,256]{1,0:T(8,128)S(1)}, f3...) conditional(s32[]{:T(128)} %convert_element_type.31, (f32[1,2,256,256]{3,2,1,0:T(8,128)S(1)}, ...), branch_computations={%region_6.7_spmd, %region_7.8_spmd} | conditional | flops 2016022016 | bytes 16538672 | solution.py:130
  126.1 1.6 convolution_bitcast_fusion.7
  127.7 2.4 %fusion.151 = f32[1,2,256,256]{3,2,1,0:T(8,128)} fusion(f32[1,2,256,256]{3,2,1,0:T(8,128)S(1)} %get-tuple-element.134, f32[2,256,256]{2,1,0:T(8,128)S(1)} %convolution_bitcast_fusion.7, f32[256,256]{1,0:T(8,128)} %get-tuple-element.135), kind=kOutput, calls=%fused_computation.238 | convolution fusion | flops 402784256 | bytes 1835008 | tf_op jit(solution)/shard_map/cond/branch_1_fun/dot_general | solution.py:115
  130.0 17.2 %copy.48 = f32[2,256,256]{0,2,1:T(8,128)} copy(f32[2,256,256]{2,1,0:T(8,128)} %bitcast.86) | data formatting | bytes 1048576 | tf_op jit(solution)/shard_map/cond/branch_1_fun/sub | solution.py:118
  147.2 2.3 %gather_fusion.3 = f32[256,2]{1,0:T(8,128)S(1)} fusion(f32[2,256,256]{0,2,1:T(8,128)} %copy.48, s32[256]{0:T(256)S(1)} %bitcast.445), kind=kCustom, calls=%fused_computation.3 | custom fusion | bytes 6144 | tf_op jit(solution)/shard_map/cond/branch_1_fun/jit(diagonal)/gather | solution.py:66
  149.5 0.3 divide_reduce_fusion.7
  149.9 1.2 fusion.157
  151.2 1.3 fusion.170
  152.5 1.3 fusion.167
  153.9 1.4 fusion.154
  155.4 0.4 fusion.159
  155.7 1.1 fusion.257
  156.8 1.1 fusion.152
  158.0 1.1 pad_maximum_fusion.3
  159.0 1.0 copy.105
  160.0 0.9 copy.104
  160.9 4.6 %fusion.205 = f32[1,2,256,32]{3,1,2,0:T(2,128)S(1)} fusion(s32[256,32]{1,0:T(8,128)S(1)} %copy.49, f32[2,256,256]{2,1,0:T(8,128)S(1)} %bitcast.446), kind=kOutput, calls=%fused_computation.317 | convolution fusion | flops 52428800 | bytes 622592 | tf_op jit(solution)/shard_map/ecij,ikj->ecik/dot_general | solution.py:138
  165.6 0.1 reshape_reshape.3
  165.7 8.4 %all_to_all.28 = f32[32,2,1,2,128]{4,0,3,2,1:T(8,128)S(1)} all-to-all(f32[32,2,1,2,128]{4,0,3,2,1:T(8,128)S(1)} %copy.53), channel_id=1, replica_groups=mesh['slab'=4,'energy_0'=4,'energy_1'=8,'energy_2'=2] {'energy_2'}, dimensions={1} | all-to-all | bytes 131072 | tf_op jit(solution)/shard_map/all_to_all | solution.py:38
  174.1 0.7 copy.54
  174.8 17.1 %all-to-all-start.1 = ((f32[32,2,1,2,128]{4,1,3,2,0:T(2,128)}), f32[32,2,1,2,128]{4,1,3,2,0:T(2,128)S(1)}, u32[]{:S(2)}, u32[]{:S(2)}) async-start(f32[32,2,1,2,128]{4,1,3,2,0:T(2,128)} %copy.54), calls=%async_computation.1 | async-start | bytes 131072 | tf_op jit(solution)/shard_map/all_to_all | solution.py:38
  191.9 8.9 %all-to-all-done.1 = f32[32,2,1,2,128]{4,1,3,2,0:T(2,128)S(1)} async-done(((f32[32,2,1,2,128]{4,1,3,2,0:T(2,128)}), f32[32,2,1,2,128]{4,1,3,2,0:T(2,128)S(1)}, u32[]{:S(2)}, u32[]{:S(2)}) %all-to-all-start.1) | async-done | bytes 65568 | tf_op jit(solution)/shard_map/all_to_all | solution.py:38
  200.9 0.0 copy-done
  200.9 0.3 convolution_bitcast_fusion.10
  201.2 0.3 convolution_bitcast_fusion.8
  201.6 0.3 fusion.211
  201.9 0.3 fusion.213
  202.3 0.1 copy.56
  202.4 14.8 %all_to_all.29 = f32[64,2,128]{2,1,0:T(2,128)S(1)} all-to-all(f32[64,2,128]{2,1,0:T(2,128)S(1)} %copy.56), channel_id=1, replica_groups=mesh['slab'=4,'energy_0'=4,'energy_1'=8,'energy_2'=2] {'energy_0','energ..., dimensions={0} | all-to-all | bytes 131072 | tf_op jit(solution)/shard_map/all_to_all | solution.py:150
  217.2 0.1 reshape.5976
  217.3 4.5 %copy_subtract_fusion = f32[1,2,256,256]{3,1,2,0:T(2,128)S(1)} fusion(f32[1,2,256,256]{3,2,1,0:T(8,128)} %get-tuple-element.154, f32[2,256,32]{2,1,0:T(8,128)S(1)} %reshape.5976, s32[256,32]{1,0:T(8,128)S(1)} %copy.49), kind=kOutput, calls=%fused_computation.335 | convolution fusion | flops 52559872 | bytes 1146880 | tf_op jit(solution)/shard_map/ecik,ikj->ecij/dot_general | solution.py:152
  221.8 0.5 slice_add_fusion.15
  222.3 0.4 fusion.220
  222.7 0.4 fusion.217
  223.1 1.4 fusion.209
  224.6 0.4 fusion.226
  225.0 0.4 fusion.224
  225.4 1.4 fusion.207
  226.8 0.8 pad_maximum_fusion.5
  227.7 0.6 copy.110
  (19 shorter events, 0.4 us)
Async XLA Ops:
  3.9 14.7 %collective-permute-start = (f32[1,2,256,256]{3,2,1,0:T(8,128)S(1)}, f32[1,2,256,256]{3,2,1,0:T(8,128)S(1)}, u32[]{:S(2)}, u32[]{:S(2)}) collective-permute-start(f32[1,2,256,256]{3,2,1,0:T(8,128)S(1)} %get-tuple-element.149), channel_id=1, source_target_pairs={{0,64},{64,128},{128,192},{1,65},{65,129},{129,193},{2,66},{66,130... | collective-permute-start | bytes 1572872 | tf_op jit(solution)/shard_map/ppermute | solution.py:20
  18.6 15.4 %copy-start.1 = (s32[256,32]{0,1:T(8,128)S(1)}, s32[256,32]{0,1:T(8,128)}, u32[]{:S(2)}) copy-start(s32[256,32]{0,1:T(8,128)} %param.30) | copy-start | bytes 98308
  18.6 15.5 %copy-start.2 = (s32[256,32]{0,1:T(8,128)S(1)}, s32[256,32]{0,1:T(8,128)}, u32[]{:S(2)}) copy-start(s32[256,32]{0,1:T(8,128)} %param.31) | copy-start | bytes 98308
  18.6 14.0 %collective-permute-start.1 = (f32[1,2,256,256]{3,2,1,0:T(8,128)S(1)}, f32[1,2,256,256]{3,2,1,0:T(8,128)S(1)}, u32[]{:S(2)}, u32[]{:S(2)}) collective-permute-start(f32[1,2,256,256]{3,2,1,0:T(8,128)S(1)} %get-tuple-element.150), channel_id=1, source_target_pairs={{0,64},{64,128},{128,192},{1,65},{65,129},{129,193},{2,66},{66,130... | collective-permute-start | bytes 1572872 | tf_op jit(solution)/shard_map/ppermute | solution.py:20
  32.5 168.3 %copy-start = (f32[2,6,64,64]{3,2,1,0:T(8,128)S(1)}, f32[2,6,64,64]{3,2,1,0:T(8,128)}, u32[]{:S(2)}) copy-start(f32[2,6,64,64]{3,2,1,0:T(8,128)} %param.29) | copy-start | bytes 589828
  32.5 93.6 %collective-permute-start.2 = (f32[1,2,256,256]{3,2,1,0:T(8,128)S(1)}, f32[1,2,256,256]{3,2,1,0:T(8,128)S(1)}, u32[]{:S(2)}, u32[]{:S(2)}) collective-permute-start(f32[1,2,256,256]{3,2,1,0:T(8,128)S(1)} %get-tuple-element.151), channel_id=1, source_target_pairs={{0,64},{64,128},{128,192},{1,65},{65,129},{129,193},{2,66},{66,130... | collective-permute-start | bytes 1572872 | tf_op jit(solution)/shard_map/ppermute | solution.py:20
  174.8 26.1 %all-to-all-start.1 = ((f32[32,2,1,2,128]{4,1,3,2,0:T(2,128)}), f32[32,2,1,2,128]{4,1,3,2,0:T(2,128)S(1)}, u32[]{:S(2)}, u32[]{:S(2)}) async-start(f32[32,2,1,2,128]{4,1,3,2,0:T(2,128)} %copy.54), calls=%async_computation.1 | async-start | bytes 131072 | tf_op jit(solution)/shard_map/all_to_all | solution.py:38
where the time goes:
time: 229 us; the launch traced here: 228 us
  waiting for transfers between devices  127 us (55%)
  matrix products  25.5 us (11%)
  local copies, waits for them, and re-layouts  24.3 us (11%)
  blocking collectives  23.2 us (10%)
  starting transfers between devices  21.2 us (9%)
  other arithmetic  5.22 us (2%)
    ppermute x3, waiting for transfers between devices, shifted_2(): return lax.ppermute(block, axis, route)  118 us
    sub x1, local copies, waits for them, and re-layouts, advance(): schur_new = shifted - through  17.2 us
    all_to_all x1, starting transfers between devices, exchange_in_order(): whole = lax.all_to_all(whole, axes[k], k, k, tiled=True)  17.1 us
    all_to_all x1, blocking collectives, body(): lax.all_to_all(owned, ENERGY, split_axis=0, concat_axis=2, tiled=True)  14.8 us
    all_to_all x1, waiting for transfers between devices, exchange_in_order(): whole = lax.all_to_all(whole, axes[k], k, k, tiled=True)  8.95 us
    all_to_all x1, blocking collectives, exchange_in_order(): whole = lax.all_to_all(whole, axes[k], k, k, tiled=True)  8.38 us
    dot_general x4, matrix products, complex_product(): jnp.matmul(left_real + left_imag, right_real + right_imag, precision=HIGH...  5.39 us
    dot_general x1, matrix products, body(): jnp.einsum('ecij,ikj->ecik', inverse, pair_mask, precision=HIGHEST)  4.6 us
  transfers between devices with their start and end apart: 4, of which 4 were waited for; matrix products, arithmetic and copies ran while one was open for 0% of the time, Pallas kernels for 0%

commit v1 on v0

v1 whole, which is shorter than its diff:
```python
import functools
import math

import jax
import jax.numpy as jnp
from jax import lax
from jax.experimental import pallas as pl
from jax.experimental.pallas import tpu as pltpu
from jax.sharding import Mesh
from jax.sharding import PartitionSpec as P

B = 256
HALF = B // 2
NEIGH = 32
ENERGY = ("y", "z", "core")
PACKED_H = HALF + 16
PAYLOAD = PACKED_H + B
PIECE = PAYLOAD // 2
GROUPS = 4
ROWS = B // GROUPS
F32 = jnp.float32
BF16 = jnp.bfloat16
VMEM = pl.BlockSpec(memory_space=pltpu.VMEM)
SMEM = pl.BlockSpec(memory_space=pltpu.SMEM)


def iota(shape, dim):
    return lax.broadcasted_iota(jnp.int32, shape, dim)


def split(x):
    high = x.astype(BF16)
    return high, (x - high.astype(F32)).astype(BF16)


def left_real(x):
    high, low = split(x)
    return jnp.concatenate([high, high, low], axis=1)


def left_complex(real, imag):
    return jnp.concatenate([left_real(real), left_real(imag)], axis=1)


def right_real(real, imag):
    real_high, real_low = split(real)
    imag_high, imag_low = split(imag)
    high = jnp.concatenate([real_high, imag_high], axis=1)
    low = jnp.concatenate([real_low, imag_low], axis=1)
    return jnp.concatenate([high, low, high], axis=0)


def right_complex(real, imag):
    return jnp.concatenate([right_real(real, imag), right_real(-imag, real)], axis=0)


def product(left, right):
    both = jnp.dot(left, right, preferred_element_type=F32)
    return both[:, :B], both[:, B:]


def pack_body(h_ref, c_ref, head_ref, piece_ref, payload):
    row = iota((HALF, HALF), 0)
    col = iota((HALF, HALF), 1)
    lower = h_ref[HALF:, HALF:]
    payload[:HALF, :HALF] = jnp.where(row <= col, h_ref[:HALF, :HALF], lower)
    payload[:HALF, HALF:] = h_ref[:HALF, HALF:]
    diagonal = jnp.sum(jnp.where(row == col, lower, 0.0), axis=0, keepdims=True)
    payload[HALF:PACKED_H, :HALF] = jnp.broadcast_to(diagonal, (PACKED_H - HALF, HALF))
    payload[HALF:PACKED_H, HALF:] = jnp.zeros((PACKED_H - HALF, HALF), F32)
    payload[PACKED_H:, :] = c_ref[...]
    head_ref[...] = payload[:PACKED_H, :]
    start = pl.multiple_of(lax.axis_index("core") * PIECE, 8)
    piece_ref[...] = payload[pl.ds(start, PIECE), :]


def pack(hamiltonian, coupling):
    return pl.pallas_call(
        pack_body,
        out_shape=(
            jax.ShapeDtypeStruct((PACKED_H, B), F32),
            jax.ShapeDtypeStruct((PIECE, B), F32),
        ),
        in_specs=[VMEM, VMEM],
        out_specs=(VMEM, VMEM),
        scratch_shapes=[pltpu.VMEM((PAYLOAD, B), F32)],
        name="pack",
    )(hamiltonian, coupling)


def unpack_h(packed_ref, h):
    row = iota((HALF, HALF), 0)
    col = iota((HALF, HALF), 1)
    mixed = packed_ref[:HALF, :HALF]
    turned = mixed.T
    across = packed_ref[:HALF, HALF:]
    h[:HALF, :HALF] = jnp.where(row <= col, mixed, turned)
    h[:HALF, HALF:] = across
    h[HALF:, :HALF] = across.T
    last = jnp.where(row > col, mixed, turned)
    diagonal = packed_ref[HALF : HALF + 1, :HALF]
    h[HALF:, HALF:] = jnp.where(row == col, diagonal, last)


def stage_math(stage, e_ref, eta_ref, h, c, g_in, g_out, p_out):
    row = iota((B, B), 0)
    col = iota((B, B), 1)
    on = row == col

    def finish(negated_real, negated_imag):
        full_real = jnp.where(on, e_ref[0], 0.0) - negated_real
        diag_real = jnp.sum(jnp.where(on, full_real, 0.0), axis=0, keepdims=True)
        side_real = jnp.sum(jnp.where(on, full_real, 0.0), axis=1, keepdims=True)
        if negated_imag is None:
            diag_imag = jnp.full((1, B), eta_ref[0], F32)
            side_imag = jnp.full((B, 1), eta_ref[0], F32)
        else:
            full_imag = jnp.where(on, eta_ref[0], 0.0) - negated_imag
            diag_imag = jnp.sum(jnp.where(on, full_imag, 0.0), axis=0, keepdims=True)
            side_imag = jnp.sum(jnp.where(on, full_imag, 0.0), axis=1, keepdims=True)

        def reciprocal(real, imag):
            modulus = real * real + imag * imag
            return real / modulus, -imag / modulus

        row_real, row_imag = reciprocal(diag_real, diag_imag)
        col_real, col_imag = reciprocal(side_real, side_imag)
        n_real = jnp.where(on, 0.0, -negated_real)
        outer_real = col_real * row_real - col_imag * row_imag
        outer_imag = col_real * row_imag + col_imag * row_real
        if negated_imag is None:
            z_real = outer_real * n_real
            z_imag = outer_imag * n_real
            p_real, p_imag = product(left_real(n_real), right_real(z_real, z_imag))
        else:
            n_imag = jnp.where(on, 0.0, -negated_imag)
            z_real = outer_real * n_real - outer_imag * n_imag
            z_imag = outer_real * n_imag + outer_imag * n_real
            p_real, p_imag = product(left_complex(n_real, n_imag), right_complex(z_real, z_imag))
        x_real = jnp.where(on, row_real, 0.0) - z_real
        x_imag = jnp.where(on, row_imag, 0.0) - z_imag
        add_real, add_imag = product(left_complex(x_real, x_imag), right_complex(p_real, p_imag))
        g_out[0] = x_real + add_real
        g_out[1] = x_imag + add_imag
        if p_out is not None:
            p_out[0] = p_real
            p_out[1] = p_imag

    @pl.when(stage == 0)
    def _():
        finish(h[...], None)

    if g_in is not None:

        @pl.when(stage > 0)
        def _():
            c_high, c_low = split(c[...])
            left = jnp.concatenate([c_high, c_high, c_low], axis=1)
            t_real, t_imag = product(left, right_real(g_in[0], g_in[1]))
            through = jnp.concatenate([left_real(t_real), left_real(t_imag)], axis=0)
            right = jnp.concatenate([c_high, c_low, c_high], axis=1)
            u = lax.dot_general(through, right, (((1,), (1,)), ((), ())), preferred_element_type=F32)
            finish(h[...] + u[:B], u[B:])


def first_body(e_ref, eta_ref, head_ref, g_out, h):
    stage = lax.axis_index("slab") - 3

    @pl.when(stage >= 0)
    def _():
        unpack_h(head_ref, h)
        stage_math(stage, e_ref, eta_ref, h, None, None, g_out, None)


def middle_body(distance, e_ref, eta_ref, mine_ref, other_ref, g_in, g_out, payload, h):
    stage = lax.axis_index("slab") - distance

    @pl.when(stage >= 0)
    def _():
        core = lax.axis_index("core")
        payload[pl.ds(pl.multiple_of(core * PIECE, 8), PIECE), :] = mine_ref[...]
        payload[pl.ds(pl.multiple_of((1 - core) * PIECE, 8), PIECE), :] = other_ref[...]
        unpack_h(payload, h)
        stage_math(stage, e_ref, eta_ref, h, payload.at[PACKED_H:, :], g_in, g_out, None)


def along_lanes(x, index):
    return jnp.take_along_axis(x, index, axis=1)


def last_body(e_ref, eta_ref, h_ref, c_ref, g_in, near_ref, g_out, p_out, pair_out, halves):
    stage_math(lax.axis_index("slab"), e_ref, eta_ref, h_ref, c_ref, g_in, g_out, p_out)
    near = near_ref[...]
    inside = jnp.bitwise_and(near, HALF - 1)
    upper = near >= HALF
    group = iota((ROWS, 128), 1) // NEIGH
    for part in range(2):
        halves[0] = g_out[part, :, :HALF]
        halves[1] = g_out[part, :, HALF:]
        result = jnp.zeros((ROWS, 128), F32)
        for q in range(GROUPS):
            left = halves[0, pl.ds(q, ROWS, stride=GROUPS), :]
            right = halves[1, pl.ds(q, ROWS, stride=GROUPS), :]
            picked = jnp.where(upper, along_lanes(right, inside), along_lanes(left, inside))
            result = jnp.where(group == q, picked, result)
        pair_out[:, part, :] = result


G_SHAPE = jax.ShapeDtypeStruct((2, B, B), F32)


def first(e, eta, head):
    return pl.pallas_call(
        first_body,
        out_shape=G_SHAPE,
        in_specs=[SMEM, SMEM, VMEM],
        out_specs=VMEM,
        scratch_shapes=[pltpu.VMEM((B, B), F32)],
        name="first",
    )(e, eta, head)


def middle(distance, e, eta, mine, other, g):
    return pl.pallas_call(
        functools.partial(middle_body, distance),
        out_shape=G_SHAPE,
        in_specs=[SMEM, SMEM, VMEM, VMEM, VMEM],
        out_specs=VMEM,
        scratch_shapes=[pltpu.VMEM((PAYLOAD, B), F32), pltpu.VMEM((B, B), F32)],
        name="middle",
    )(e, eta, mine, other, g)


def last(e, eta, hamiltonian, coupling, g, near):
    return pl.pallas_call(
        last_body,
        out_shape=(G_SHAPE, G_SHAPE, jax.ShapeDtypeStruct((ROWS, 2, 128), F32)),
        in_specs=[SMEM, SMEM, VMEM, VMEM, VMEM, VMEM],
        out_specs=(VMEM, VMEM, VMEM),
        scratch_shapes=[pltpu.VMEM((2, B, HALF), F32)],
        name="last",
    )(e, eta, hamiltonian, coupling, g, near)


def tables_body(near_ref, mode_ref, d_ref, near_out, mode_out, inverse_out, next_out, rounds_out, weight_out, wide):
    wide[0, :, :NEIGH] = near_ref[...]
    wide[1, :, :NEIGH] = mode_ref[...]
    near_parts, mode_parts = (
        [wide[w, pl.ds(q, ROWS, stride=GROUPS), :][:, :NEIGH] for q in range(GROUPS)] for w in range(2)
    )
    near = jnp.concatenate(near_parts, axis=1)
    near_out[...] = near
    modes = jnp.concatenate(mode_parts, axis=1)
    y, z, core = (lax.axis_index(a) for a in ENERGY)
    mine = (y * lax.axis_size("z") + z) * lax.axis_size("core") + core
    own = jnp.where(iota((ROWS, 128), 0) == mine, modes, 0)
    mode_out[...] = jnp.broadcast_to(jnp.sum(own, axis=0, keepdims=True), (8, 128))
    column = iota((ROWS, B), 1)
    for q in range(GROUPS):
        table = jnp.full((ROWS, B), -1, jnp.int32)
        for k in reversed(range(NEIGH)):
            table = jnp.where(near_parts[q][:, k : k + 1] == column, q * NEIGH + k, table)
        inverse_out[q * ROWS : (q + 1) * ROWS, :] = table
    lane = iota((ROWS, 128), 1)
    place = jnp.bitwise_and(lane, NEIGH - 1)
    follower = jnp.full((ROWS, 128), -1, jnp.int32)
    count = jnp.zeros((ROWS, 128), F32)
    for shift in reversed(range(1, NEIGH)):
        same = (pltpu.roll(near, 128 - shift, axis=1) == near) & (place + shift < NEIGH)
        follower = jnp.where(same, lane + shift, follower)
        count = count + jnp.where(same, 1.0, 0.0)
    next_out[...] = follower
    rounds_out[0] = jnp.max(count).astype(jnp.int32)
    scale = 2.0 * math.sqrt(B / NEIGH)
    modes_count, energies = d_ref.shape[1], d_ref.shape[2]
    size = 2 * energies
    total = modes_count * size
    for m in range(modes_count):
        real = scale * d_ref[0, m]
        imag = scale * d_ref[1, m]
        top = jnp.concatenate([real, -imag], axis=1)
        bottom = jnp.concatenate([imag, real], axis=1)
        high, low = split(jnp.concatenate([top, bottom], axis=0))
        weight_out[:, m * size : (m + 1) * size] = high
        weight_out[:, total + m * size : total + (m + 1) * size] = high
        weight_out[:, 2 * total + m * size : 2 * total + (m + 1) * size] = low


def tables(neighbors, phonon_modes, propagator):
    modes_count, energies = propagator.shape[1:3]
    return pl.pallas_call(
        tables_body,
        out_shape=(
            jax.ShapeDtypeStruct((ROWS, 128), jnp.int32),
            jax.ShapeDtypeStruct((8, 128), jnp.int32),
            jax.ShapeDtypeStruct((B, B), jnp.int32),
            jax.ShapeDtypeStruct((ROWS, 128), jnp.int32),
            jax.ShapeDtypeStruct((1,), jnp.int32),
            jax.ShapeDtypeStruct((2 * energies, 6 * modes_count * energies), BF16),
        ),
        in_specs=[VMEM, VMEM, VMEM],
        out_specs=(VMEM, VMEM, VMEM, VMEM, SMEM, VMEM),
        scratch_shapes=[pltpu.VMEM((2, B, 128), jnp.int32)],
        name="tables",
    )(neighbors, phonon_modes, propagator)


def convolve_body(modes_count, weight_ref, mode_ref, green_ref, out_ref):
    stacked = jnp.concatenate([green_ref[:, 0, :], green_ref[:, 1, :]], axis=0)
    high, low = (x.astype(F32) for x in split(stacked))
    mode = mode_ref[0:1, :]
    highs, lows = [], []
    for m in range(modes_count):
        highs.append(jnp.where(mode == m, high, 0.0).astype(BF16))
        lows.append(jnp.where(mode == m, low, 0.0).astype(BF16))
    right = jnp.concatenate(highs + lows + highs, axis=0)
    result = jnp.dot(weight_ref[...], right, preferred_element_type=F32)
    energies = green_ref.shape[0]
    out_ref[:, 0, :] = result[:energies]
    out_ref[:, 1, :] = result[energies:]


def convolve(modes_count, weight, mode, green):
    return pl.pallas_call(
        functools.partial(convolve_body, modes_count),
        out_shape=jax.ShapeDtypeStruct(green.shape, F32),
        in_specs=[VMEM, VMEM, VMEM],
        out_specs=VMEM,
        name="convolve",
    )(weight, mode, green)


def correct_body(rounds_ref, self_ref, next_ref, inverse_ref, g_ref, p_ref, out_ref, moved):
    part_real = self_ref[:, 0, :]
    part_imag = self_ref[:, 1, :]
    follower = next_ref[...]

    def gather_round(_, carry):
        sum_real, sum_imag, pointer = carry
        valid = pointer >= 0
        index = jnp.maximum(pointer, 0)
        sum_real = sum_real + jnp.where(valid, along_lanes(part_real, index), 0.0)
        sum_imag = sum_imag + jnp.where(valid, along_lanes(part_imag, index), 0.0)
        return sum_real, sum_imag, jnp.where(valid, along_lanes(follower, index), -1)

    sum_real, sum_imag, _ = lax.fori_loop(
        0, rounds_ref[0], gather_round, (part_real, part_imag, follower)
    )
    reals, imags = [], []
    for q in range(GROUPS):
        row_real, row_imag = [], []
        for side in range(2):
            table = inverse_ref[q * ROWS : (q + 1) * ROWS, side * HALF : (side + 1) * HALF]
            valid = table >= 0
            index = jnp.maximum(table, 0)
            row_real.append(jnp.where(valid, along_lanes(sum_real, index), 0.0))
            row_imag.append(jnp.where(valid, along_lanes(sum_imag, index), 0.0))
        reals.append(jnp.concatenate(row_real, axis=1))
        imags.append(jnp.concatenate(row_imag, axis=1))
    sigma_real = jnp.concatenate(reals, axis=0)
    sigma_imag = jnp.concatenate(imags, axis=0)
    g_real, g_imag = g_ref[0], g_ref[1]
    s_real, s_imag = product(left_complex(sigma_real, sigma_imag), right_complex(g_real, g_imag))
    for q in range(GROUPS):
        rows = slice(q * ROWS, (q + 1) * ROWS)
        for part, value in enumerate((s_real, s_imag)):
            for side in range(2):
                piece = value[rows, side * HALF : (side + 1) * HALF]
                moved[2 * part + side, pl.ds(q, ROWS, stride=GROUPS), :] = piece
    moved_real = jnp.concatenate([moved[0], moved[1]], axis=1)
    moved_imag = jnp.concatenate([moved[2], moved[3]], axis=1)
    p_real, p_imag = p_ref[0], p_ref[1]
    square_real, square_imag = product(left_complex(p_real, p_imag), right_complex(p_real, p_imag))
    add_real, add_imag = product(
        left_complex(g_real, g_imag),
        right_complex(square_real + moved_real, square_imag + moved_imag),
    )
    out_ref[0, 0] = g_real + add_real
    out_ref[0, 1] = g_imag + add_imag


def correct(rounds, self_part, follower, inverse, g, p):
    return pl.pallas_call(
        correct_body,
        out_shape=jax.ShapeDtypeStruct((1, 2, B, B), F32),
        in_specs=[SMEM, VMEM, VMEM, VMEM, VMEM, VMEM],
        out_specs=VMEM,
        scratch_shapes=[pltpu.VMEM((4, B, HALF), F32)],
        name="correct",
    )(rounds, self_part, follower, inverse, g, p)


def body(energies, broadening, hamiltonian, coupling, propagator, neighbors, phonon_modes):
    swap = [(0, 1), (1, 0)]
    head, piece = pack(hamiltonian, coupling)
    head0 = lax.ppermute(head, "slab", [(0, 3)])
    far = lax.ppermute(piece, "slab", [(0, 2), (1, 3)])
    near_piece = lax.ppermute(piece, "slab", [(0, 1), (1, 2), (2, 3)])
    far_other = lax.ppermute(far, "core", swap)
    near_other = lax.ppermute(near_piece, "core", swap)
    near, mode, inverse, follower, rounds, weight = tables(neighbors, phonon_modes, propagator)
    g = first(energies, broadening, head0)
    g = middle(2, energies, broadening, far, far_other, g)
    g = middle(1, energies, broadening, near_piece, near_other, g)
    g, p, pairs = last(energies, broadening, hamiltonian, coupling, g, near)
    regrouped = lax.all_to_all(pairs, ENERGY, 0, 0, tiled=True)
    owned = convolve(propagator.shape[1], weight, mode, regrouped)
    returned = lax.all_to_all(owned, ENERGY, 0, 0, tiled=True)
    green = correct(rounds, returned, follower, inverse, g, p)
    self_part = jnp.swapaxes(returned, 0, 1).reshape(1, 2, B * NEIGH)
    return green, self_part


def solution(mesh):
    finer = Mesh(mesh.devices.reshape(mesh.shape["slab"], 4, 8, 2), ("slab", *ENERGY))
    in_specs = (
        P(ENERGY),
        P(ENERGY),
        P("slab", None),
        P("slab", None),
        P(),
        P("slab", None),
        P("slab", None),
    )
    out_specs = (P(ENERGY, None, "slab", None), P(ENERGY, None, "slab"))
    return jax.shard_map(body, mesh=finer, in_specs=in_specs, out_specs=out_specs, check_vma=False)
```

time: 229 us -> 86 us (0.38)
  waiting for transfers between devices: 127 us -> 7.77 us
  Pallas kernels: 0 us -> 28.5 us
  matrix products: 25.5 us -> 0 us
  local copies, waits for them, and re-layouts: 24.3 us -> 4.2 us
  starting transfers between devices: 21.2 us -> 5.48 us
  blocking collectives: 23.2 us -> 37.4 us
  other arithmetic: 5.22 us -> 0 us
    ppermute x3 -> x5, waiting for transfers between devices: 118 us -> 7.77 us  [the longest x1 6.97 us: body(): far = lax.ppermute(piece, 'slab', [(0, 2), (1, 3)])]
    pallas_call x0 -> x8, Pallas kernels: none -> 28.5 us  [the longest x2 8.33 us: middle(): pl.pallas_call(functools.partial(middle_body, distance), out_shape=G_SHAP...]
    dot_general x20 -> x0, matrix products: 25.5 us -> none  [the longest x4 5.39 us: complex_product(): jnp.matmul(left_real + left_imag, right_real + right_imag, precision=HIGH...]
    sub x1 -> x0, local copies, waits for them, and re-layouts: 17.2 us -> none  [advance(): schur_new = shifted - through]
    all_to_all x1 -> x0, starting transfers between devices: 17.1 us -> none  [exchange_in_order(): whole = lax.all_to_all(whole, axes[k], k, k, tiled=True)]
    all_to_all x2, blocking collectives: 23.2 us -> 37.4 us  [the longest x1 22.4 us: body(): regrouped = lax.all_to_all(pairs, ENERGY, 0, 0, tiled=True)]
    all_to_all x1 -> x0, waiting for transfers between devices: 8.95 us -> none  [exchange_in_order(): whole = lax.all_to_all(whole, axes[k], k, k, tiled=True)]
    unnamed x9 -> x19, local copies, waits for them, and re-layouts: 0.83 us -> 4.2 us
  transfers between devices with their start and end apart: 4 -> 5, of which waited for: 4 -> 2; matrix products, arithmetic and copies ran while one was open for 0% -> 2% of each run, Pallas kernels for 0% -> 13%
where the time goes in v1:
time: 86 us; the launch traced here: 85.4 us
  blocking collectives  37.4 us (43%)
  Pallas kernels  28.5 us (33%)
  waiting for transfers between devices  7.77 us (9%)
  starting transfers between devices  5.48 us (6%)
  local copies, waits for them, and re-layouts  4.2 us (5%)
  between operations  2.01 us (2%)
    all_to_all x1, blocking collectives, body(): regrouped = lax.all_to_all(pairs, ENERGY, 0, 0, tiled=True)  22.4 us
    all_to_all x1, blocking collectives, body(): returned = lax.all_to_all(owned, ENERGY, 0, 0, tiled=True)  15 us
    pallas_call x2, Pallas kernels, middle(): pl.pallas_call(functools.partial(middle_body, distance), out_shape=G_SHAP...  8.33 us
    ppermute x1, waiting for transfers between devices, body(): far = lax.ppermute(piece, 'slab', [(0, 2), (1, 3)])  6.97 us
    pallas_call x1, Pallas kernels, correct(): pl.pallas_call(correct_body, out_shape=jax.ShapeDtypeStruct((1, 2, B, B),...  4.8 us
    pallas_call x1, Pallas kernels, last(): pl.pallas_call(last_body, out_shape=(G_SHAPE, G_SHAPE, jax.ShapeDtypeStru...  4.46 us
    unnamed x19, local copies, waits for them, and re-layouts  4.2 us
    pallas_call x1, Pallas kernels, tables(): pl.pallas_call(tables_body, out_shape=(jax.ShapeDtypeStruct((ROWS, 128),...  4.12 us
  transfers between devices with their start and end apart: 5, of which 2 were waited for; matrix products, arithmetic and copies ran while one was open for 2% of the time, Pallas kernels for 13%

profile of v1, /device:TPU:7, one launch (start us, length us, event | category | flops | bytes accessed | tf_op | source)
XLA Modules:
  0.0 85.4 jit_solution(8631033762327496063)
XLA Ops:
  0.6 0.0 copy-start.6
  0.6 1.8 %pack.1 = (f32[144,256]{1,0:T(8,128)}, f32[200,256]{1,0:T(8,128)}) custom-call(f32[256,256]{1,0:T(8,128)} %h_ref.3, f32[256,256]{1,0:T(8,128)} %c_ref.3), custom_call_target="tpu_custom_call" | custom-call | tf_op jit(solution)/shard_map/pack/pallas_call | solution.py:78
  2.4 1.3 %collective-permute-start.2 = (f32[200,256]{1,0:T(8,128)}, f32[200,256]{1,0:T(8,128)S(1)}, u32[]{:S(2)}, u32[]{:S(2)}) collective-permute-start(f32[200,256]{1,0:T(8,128)} %get-tuple-element.16), channel_id=1, source_target_pairs={{0,128},{64,192},{1,129},{65,193},{2,130},{66,194},{3,131},{67,195... | collective-permute-start | bytes 614408 | tf_op jit(solution)/shard_map/ppermute | solution.py:397
  3.7 1.3 %collective-permute-start = (f32[200,256]{1,0:T(8,128)}, f32[200,256]{1,0:T(8,128)S(1)}, u32[]{:S(2)}, u32[]{:S(2)}) collective-permute-start(f32[200,256]{1,0:T(8,128)} %get-tuple-element.16), channel_id=1, source_target_pairs={{0,64},{64,128},{128,192},{1,65},{65,129},{129,193},{2,66},{66,130... | collective-permute-start | bytes 614408 | tf_op jit(solution)/shard_map/ppermute | solution.py:398
  5.0 7.0 %collective-permute-done.2.mine_ref = f32[200,256]{1,0:T(8,128)S(1)} collective-permute-done((f32[200,256]{1,0:T(8,128)}, f32[200,256]{1,0:T(8,128)S(1)}, u32[]{:S(2)}, u32[]{:S(2)}) %collective-permute-start.2) | collective-permute-done | bytes 204832 | tf_op jit(solution)/shard_map/ppermute | solution.py:397
  12.0 0.0 copy-start.2
  12.0 1.5 %collective-permute-start.3 = (f32[200,256]{1,0:T(8,128)S(1)}, f32[200,256]{1,0:T(8,128)S(1)}, u32[]{:S(2)}, u32[]{:S(2)}) collective-permute-start(f32[200,256]{1,0:T(8,128)S(1)} %collective-permute-done.2.mine_ref), channel_id=1, source_target_pairs={{0,1},{1,0},{2,3},{3,2},{4,5},{5,4},{6,7},{7,6},{8,9},{9,8},{10,11... | collective-permute-start | bytes 614408 | tf_op jit(solution)/shard_map/ppermute | solution.py:399
  13.5 0.0 collective-permute-done.mine_ref
  13.5 0.0 copy-start.1
  13.5 0.1 collective-permute-start.1
  13.6 1.3 %collective-permute-start.4 = (f32[144,256]{1,0:T(8,128)}, f32[144,256]{1,0:T(8,128)S(1)}, u32[]{:S(2)}, u32[]{:S(2)}) collective-permute-start(f32[144,256]{1,0:T(8,128)} %get-tuple-element.17), channel_id=1, source_target_pairs={{0,192},{1,193},{2,194},{3,195},{4,196},{5,197},{6,198},{7,199},{8... | collective-permute-start | bytes 442376 | tf_op jit(solution)/shard_map/ppermute | solution.py:396
  16.2 0.0 copy-done.6
  16.2 0.0 copy-start.7
  16.2 0.8 copy.9.near_ref
  17.0 0.0 copy-done.7
  17.0 0.7 copy.10.mode_ref
  17.8 4.1 %tables.1 = (s32[64,128]{1,0:T(8,128)}, s32[8,128]{1,0:T(8,128)}, s32[256,256]{1,0:T(8,128)}, s32[64,128]{1,0:T(8,128)}, s32[1]{0:T(128)}, /*index=5*/bf16[128,2304]{1,0:T(8,128)(2,1)}) custom-call(s32[256,32]{1,0:T(8,128)} %copy.9.near_ref, s32[256,32]{1,0:T(8,128)} %copy.10.mode_ref, f32[2,6,64,64]{3,2,1,0:T(8,128)} %d_ref.1), custom_call_target="tpu_custom_call" | custom-call | tf_op jit(solution)/shard_map/tables/pallas_call | solution.py:291
  21.9 0.0 copy-done.2
  21.9 0.0 copy-done.1
  21.9 0.8 collective-permute-done.4.head_ref
  22.7 0.0 copy-start.5
  22.7 0.7 copy-done.5
  23.4 2.9 %first.1.g_in = f32[2,256,256]{2,1,0:T(8,128)} custom-call(f32[1]{0:T(128)S(6)} %copy.12.e_ref, f32[1]{0:T(128)S(6)} %copy.13.eta_ref, f32[144,256]{1,0:T(8,128)} %copy-done.5), custom_call_target="tpu_custom_call" | custom-call | tf_op jit(solution)/shard_map/first/pallas_call | solution.py:213
  26.3 0.0 collective-permute-done.3.other_ref
  26.3 0.0 copy-start.3
  26.3 0.7 copy-done.3
  27.0 4.2 %middle.2.g_in = f32[2,256,256]{2,1,0:T(8,128)} custom-call(f32[1]{0:T(128)S(6)} %copy.12.e_ref, f32[1]{0:T(128)S(6)} %copy.13.eta_ref, f32[200,256]{1,0:T(8,128)} %copy-done.2, f32[200,256]{1,0:T(8,128)} %copy-done.3, f32[2,256,256]{2,1,0:T(8,128)} %first.1.g_in), custom_call_target="tpu_custom_call" | custom-call | tf_op jit(solution)/shard_map/middle/pallas_call | solution.py:224
  31.1 0.0 collective-permute-done.1.other_ref
  31.1 0.0 copy-start.4
  31.1 0.7 copy-done.4
  31.8 4.2 %middle.3.g_in = f32[2,256,256]{2,1,0:T(8,128)} custom-call(f32[1]{0:T(128)S(6)} %copy.12.e_ref, f32[1]{0:T(128)S(6)} %copy.13.eta_ref, f32[200,256]{1,0:T(8,128)} %copy-done.1, f32[200,256]{1,0:T(8,128)} %copy-done.4, f32[2,256,256]{2,1,0:T(8,128)} %middle.2.g_in), custom_call_target="tpu_custom_call" | custom-call | tf_op jit(solution)/shard_map/middle/pallas_call | solution.py:224
  36.0 4.5 %last.1 = (f32[2,256,256]{2,1,0:T(8,128)}, f32[2,256,256]{2,1,0:T(8,128)}, f32[64,2,128]{2,1,0:T(2,128)}) custom-call(f32[1]{0:T(128)S(6)} %copy.12.e_ref, f32[1]{0:T(128)S(6)} %copy.13.eta_ref, f32[256,256]{1,0:T(8,128)} %h_ref.3, f32[256,256]{1,0:T(8,128)} %c_ref.3, f32[2,256,256]{2,1,0:T(8,128)} %middle.3.g_in, s32[64,128]{1,0:T(8,128)} %get-tuple-element.18.near_ref), custom_call_target="tpu_custom_call" | custom-call | tf_op jit(solution)/shard_map/last/pallas_call | solution.py:235
  40.5 22.4 %all_to_all.10.green_ref = f32[64,2,128]{2,1,0:T(2,128)} all-to-all(f32[64,2,128]{2,1,0:T(2,128)} %get-tuple-element.19), channel_id=1, replica_groups=mesh['slab'=4,'y'=4,'z'=8,'core'=2] {'y','z','core'}, dimensions={0} | all-to-all | bytes 131072 | tf_op jit(solution)/shard_map/all_to_all | solution.py:406
  62.8 2.1 %convolve.1 = f32[64,2,128]{2,1,0:T(2,128)} custom-call(bf16[128,2304]{1,0:T(8,128)(2,1)} %get-tuple-element.14.weight_ref, s32[8,128]{1,0:T(8,128)} %get-tuple-element.15.mode_ref, f32[64,2,128]{2,1,0:T(2,128)} %all_to_all.10.green_ref), custom_call_target="tpu_custom_call" | custom-call | tf_op jit(solution)/shard_map/convolve/pallas_call | solution.py:324
  64.9 15.0 %all_to_all.11.self_ref = f32[64,2,128]{2,1,0:T(2,128)} all-to-all(f32[64,2,128]{2,1,0:T(2,128)} %convolve.1), channel_id=1, replica_groups=mesh['slab'=4,'y'=4,'z'=8,'core'=2] {'y','z','core'}, dimensions={0} | all-to-all | bytes 131072 | tf_op jit(solution)/shard_map/all_to_all | solution.py:408
  79.9 0.0 copy-start
  79.9 4.8 %correct.1 = f32[1,2,256,256]{3,2,1,0:T(8,128)} custom-call(s32[1]{0:T(128)} %get-tuple-element.13.rounds_ref, f32[64,2,128]{2,1,0:T(2,128)} %all_to_all.11.self_ref, s32[64,128]{1,0:T(8,128)} %get-tuple-element.20.next_ref, s32[256,256]{1,0:T(8,128)} %get-tuple-element.21.inverse_ref, f32[2,256,256]{2,1,0:T(8,128)} %get-tuple-element.22.g_ref, ...), custom_call_target="tpu_custom_call" | custom-call | tf_op jit(solution)/shard_map/correct/pallas_call | solution.py:383
  84.7 0.0 copy-done
  84.7 0.6 copy.14
Async XLA Ops:
  0.6 15.6 %copy-start.6 = (s32[256,32]{0,1:T(8,128)S(1)}, s32[256,32]{0,1:T(8,128)}, u32[]{:S(2)}) copy-start(s32[256,32]{0,1:T(8,128)} %param.12) | copy-start | bytes 98308
  2.4 9.6 %collective-permute-start.2 = (f32[200,256]{1,0:T(8,128)}, f32[200,256]{1,0:T(8,128)S(1)}, u32[]{:S(2)}, u32[]{:S(2)}) collective-permute-start(f32[200,256]{1,0:T(8,128)} %get-tuple-element.16), channel_id=1, source_target_pairs={{0,128},{64,192},{1,129},{65,193},{2,130},{66,194},{3,131},{67,195... | collective-permute-start | bytes 614408 | tf_op jit(solution)/shard_map/ppermute | solution.py:397
  3.7 9.8 %collective-permute-start = (f32[200,256]{1,0:T(8,128)}, f32[200,256]{1,0:T(8,128)S(1)}, u32[]{:S(2)}, u32[]{:S(2)}) collective-permute-start(f32[200,256]{1,0:T(8,128)} %get-tuple-element.16), channel_id=1, source_target_pairs={{0,64},{64,128},{128,192},{1,65},{65,129},{129,193},{2,66},{66,130... | collective-permute-start | bytes 614408 | tf_op jit(solution)/shard_map/ppermute | solution.py:398
  12.0 9.9 %copy-start.2 = (f32[200,256]{1,0:T(8,128)}, f32[200,256]{1,0:T(8,128)S(1)}, u32[]{:S(2)}) copy-start(f32[200,256]{1,0:T(8,128)S(1)} %collective-permute-done.2.mine_ref) | copy-start | bytes 614404
  12.0 14.3 %collective-permute-start.3 = (f32[200,256]{1,0:T(8,128)S(1)}, f32[200,256]{1,0:T(8,128)S(1)}, u32[]{:S(2)}, u32[]{:S(2)}) collective-permute-start(f32[200,256]{1,0:T(8,128)S(1)} %collective-permute-done.2.mine_ref), channel_id=1, source_target_pairs={{0,1},{1,0},{2,3},{3,2},{4,5},{5,4},{6,7},{7,6},{8,9},{9,8},{10,11... | collective-permute-start | bytes 614408 | tf_op jit(solution)/shard_map/ppermute | solution.py:399
  13.5 8.4 %copy-start.1 = (f32[200,256]{1,0:T(8,128)}, f32[200,256]{1,0:T(8,128)S(1)}, u32[]{:S(2)}) copy-start(f32[200,256]{1,0:T(8,128)S(1)} %collective-permute-done.mine_ref) | copy-start | bytes 614404
  13.5 17.6 %collective-permute-start.1 = (f32[200,256]{1,0:T(8,128)S(1)}, f32[200,256]{1,0:T(8,128)S(1)}, u32[]{:S(2)}, u32[]{:S(2)}) collective-permute-start(f32[200,256]{1,0:T(8,128)S(1)} %collective-permute-done.mine_ref), channel_id=1, source_target_pairs={{0,1},{1,0},{2,3},{3,2},{4,5},{5,4},{6,7},{7,6},{8,9},{9,8},{10,11... | collective-permute-start | bytes 614408 | tf_op jit(solution)/shard_map/ppermute | solution.py:400
  13.6 9.1 %collective-permute-start.4 = (f32[144,256]{1,0:T(8,128)}, f32[144,256]{1,0:T(8,128)S(1)}, u32[]{:S(2)}, u32[]{:S(2)}) collective-permute-start(f32[144,256]{1,0:T(8,128)} %get-tuple-element.17), channel_id=1, source_target_pairs={{0,192},{1,193},{2,194},{3,195},{4,196},{5,197},{6,198},{7,199},{8... | collective-permute-start | bytes 442376 | tf_op jit(solution)/shard_map/ppermute | solution.py:396
  16.2 0.8 copy-start.7
  22.7 0.7 copy-start.5
  26.3 0.7 copy-start.3
  31.1 0.7 copy-start.4
  79.9 4.8 %copy-start = (f32[64,2,128]{2,1,0:T(2,128)S(1)}, f32[64,2,128]{2,1,0:T(2,128)}, u32[]{:S(2)}) copy-start(f32[64,2,128]{2,1,0:T(2,128)} %all_to_all.11.self_ref) | copy-start | bytes 196612

commit v2 on v1

--- a/solution.py
+++ b/solution.py
@@ -8,6 +8,7 @@
 from jax.experimental.pallas import tpu as pltpu
 from jax.sharding import Mesh
 from jax.sharding import PartitionSpec as P
+
 
 B = 256
 HALF = B // 2
@@ -22,6 +23,7 @@
 BF16 = jnp.bfloat16
 VMEM = pl.BlockSpec(memory_space=pltpu.VMEM)
 SMEM = pl.BlockSpec(memory_space=pltpu.SMEM)
+PARAMS = pltpu.CompilerParams(vmem_limit_bytes=16 * 1024 * 1024)
 
 
 def iota(shape, dim):
@@ -216,6 +218,7 @@
         in_specs=[SMEM, SMEM, VMEM],
         out_specs=VMEM,
         scratch_shapes=[pltpu.VMEM((B, B), F32)],
+        compiler_params=PARAMS,
         name="first",
     )(e, eta, head)
 
@@ -227,6 +230,7 @@
         in_specs=[SMEM, SMEM, VMEM, VMEM, VMEM],
         out_specs=VMEM,
         scratch_shapes=[pltpu.VMEM((PAYLOAD, B), F32), pltpu.VMEM((B, B), F32)],
+        compiler_params=PARAMS,
         name="middle",
     )(e, eta, mine, other, g)
 
@@ -238,13 +242,14 @@
         in_specs=[SMEM, SMEM, VMEM, VMEM, VMEM, VMEM],
         out_specs=(VMEM, VMEM, VMEM),
         scratch_shapes=[pltpu.VMEM((2, B, HALF), F32)],
+        compiler_params=PARAMS,
         name="last",
     )(e, eta, hamiltonian, coupling, g, near)
 
 
 def tables_body(near_ref, mode_ref, d_ref, near_out, mode_out, inverse_out, next_out, rounds_out, weight_out, wide):
-    wide[0, :, :NEIGH] = near_ref[...]
-    wide[1, :, :NEIGH] = mode_ref[...]
+    wide[0, :, :NEIGH] = near_ref[...].T
+    wide[1, :, :NEIGH] = mode_ref[...].T
     near_parts, mode_parts = (
         [wide[w, pl.ds(q, ROWS, stride=GROUPS), :][:, :NEIGH] for q in range(GROUPS)] for w in range(2)
     )
@@ -301,6 +306,7 @@
         in_specs=[VMEM, VMEM, VMEM],
         out_specs=(VMEM, VMEM, VMEM, VMEM, SMEM, VMEM),
         scratch_shapes=[pltpu.VMEM((2, B, 128), jnp.int32)],
+        compiler_params=PARAMS,
         name="tables",
     )(neighbors, phonon_modes, propagator)
 
@@ -326,11 +332,13 @@
         out_shape=jax.ShapeDtypeStruct(green.shape, F32),
         in_specs=[VMEM, VMEM, VMEM],
         out_specs=VMEM,
+        compiler_params=PARAMS,
         name="convolve",
     )(weight, mode, green)
 
 
-def correct_body(rounds_ref, self_ref, next_ref, inverse_ref, g_ref, p_ref, out_ref, moved):
+def correct_body(rounds_ref, self_ref, next_ref, inverse_ref, g_ref, p_ref, out_ref, self_out, moved):
+    self_out[...] = self_ref[...]
     part_real = self_ref[:, 0, :]
     part_imag = self_ref[:, 1, :]
     follower = next_ref[...]
@@ -382,10 +390,14 @@
 def correct(rounds, self_part, follower, inverse, g, p):
     return pl.pallas_call(
         correct_body,
-        out_shape=jax.ShapeDtypeStruct((1, 2, B, B), F32),
+        out_shape=(
+            jax.ShapeDtypeStruct((1, 2, B, B), F32),
+            jax.ShapeDtypeStruct(self_part.shape, F32),
+        ),
         in_specs=[SMEM, VMEM, VMEM, VMEM, VMEM, VMEM],
-        out_specs=VMEM,
+        out_specs=(VMEM, VMEM),
         scratch_shapes=[pltpu.VMEM((4, B, HALF), F32)],
+        compiler_params=PARAMS,
         name="correct",
     )(rounds, self_part, follower, inverse, g, p)
 
@@ -395,19 +407,19 @@
     head, piece = pack(hamiltonian, coupling)
     head0 = lax.ppermute(head, "slab", [(0, 3)])
     far = lax.ppermute(piece, "slab", [(0, 2), (1, 3)])
-    near_piece = lax.ppermute(piece, "slab", [(0, 1), (1, 2), (2, 3)])
+    close = lax.ppermute(piece, "slab", [(0, 1), (1, 2), (2, 3)])
     far_other = lax.ppermute(far, "core", swap)
-    near_other = lax.ppermute(near_piece, "core", swap)
-    near, mode, inverse, follower, rounds, weight = tables(neighbors, phonon_modes, propagator)
+    close_other = lax.ppermute(close, "core", swap)
+    near, mode, inverse, follower, rounds, weight = tables(neighbors.T, phonon_modes.T, propagator)
     g = first(energies, broadening, head0)
     g = middle(2, energies, broadening, far, far_other, g)
-    g = middle(1, energies, broadening, near_piece, near_other, g)
+    g = middle(1, energies, broadening, close, close_other, g)
     g, p, pairs = last(energies, broadening, hamiltonian, coupling, g, near)
     regrouped = lax.all_to_all(pairs, ENERGY, 0, 0, tiled=True)
     owned = convolve(propagator.shape[1], weight, mode, regrouped)
     returned = lax.all_to_all(owned, ENERGY, 0, 0, tiled=True)
-    green = correct(rounds, returned, follower, inverse, g, p)
-    self_part = jnp.swapaxes(returned, 0, 1).reshape(1, 2, B * NEIGH)
+    green, self_part = correct(rounds, returned, follower, inverse, g, p)
+    self_part = jnp.swapaxes(self_part, 0, 1).reshape(1, 2, B * NEIGH)
     return green, self_part
 
 

time: 86 us -> 70.7 us (0.82)
  Pallas kernels: 28.5 us -> 16.5 us
  local copies, waits for them, and re-layouts: 4.2 us -> 0.03 us
  waiting for transfers between devices: 7.77 us -> 10.8 us
  blocking collectives: 37.4 us -> 35.7 us
    unnamed x19 -> x10, local copies, waits for them, and re-layouts: 4.2 us -> 0.03 us
    pallas_call x2, Pallas kernels: 8.33 us -> 4.28 us  [middle(): pl.pallas_call(functools.partial(middle_body, distance), out_shape=G_SHAP...]
    ppermute x1, waiting for transfers between devices: 0.8 us -> 3.78 us  [body(): head0 = lax.ppermute(head, 'slab', [(0, 3)])]
    pallas_call x1, Pallas kernels: 4.46 us -> 2.63 us  [last(): pl.pallas_call(last_body, out_shape=(G_SHAPE, G_SHAPE, jax.ShapeDtypeStru...]
    pallas_call x1, Pallas kernels: 2.91 us -> 1.2 us  [first(): pl.pallas_call(first_body, out_shape=G_SHAPE, in_specs=[SMEM, SMEM, VMEM]...]
    pallas_call x1, Pallas kernels: 2.05 us -> 0.35 us  [convolve(): pl.pallas_call(functools.partial(convolve_body, modes_count), out_shape=j...]
    all_to_all x1, blocking collectives: 15 us -> 13.6 us  [body(): returned = lax.all_to_all(owned, ENERGY, 0, 0, tiled=True)]
    pallas_call x1, Pallas kernels: 4.12 us -> 2.75 us  [tables(): pl.pallas_call(tables_body, out_shape=(jax.ShapeDtypeStruct((ROWS, 128),...]
  transfers between devices with their start and end apart: 5 -> 5, of which waited for: 2 -> 2; matrix products, arithmetic and copies ran while one was open for 2% -> 0% of each run, Pallas kernels for 13% -> 9%
where the time goes in v2:
time: 70.7 us; the launch traced here: 70.5 us
  blocking collectives  35.7 us (50%)
  Pallas kernels  16.5 us (23%)
  waiting for transfers between devices  10.8 us (15%)
  starting transfers between devices  5.39 us (8%)
  between operations  2.09 us (3%)
    all_to_all x1, blocking collectives, body(): regrouped = lax.all_to_all(pairs, ENERGY, 0, 0, tiled=True)  22.1 us
    all_to_all x1, blocking collectives, body(): returned = lax.all_to_all(owned, ENERGY, 0, 0, tiled=True)  13.6 us
    ppermute x1, waiting for transfers between devices, body(): far = lax.ppermute(piece, 'slab', [(0, 2), (1, 3)])  6.97 us
    pallas_call x2, Pallas kernels, middle(): pl.pallas_call(functools.partial(middle_body, distance), out_shape=G_SHAP...  4.28 us
    ppermute x1, waiting for transfers between devices, body(): head0 = lax.ppermute(head, 'slab', [(0, 3)])  3.78 us
    pallas_call x1, Pallas kernels, correct(): pl.pallas_call(correct_body, out_shape=(jax.ShapeDtypeStruct((1, 2, B, B)...  3.45 us
    pallas_call x1, Pallas kernels, tables(): pl.pallas_call(tables_body, out_shape=(jax.ShapeDtypeStruct((ROWS, 128),...  2.75 us
    pallas_call x1, Pallas kernels, last(): pl.pallas_call(last_body, out_shape=(G_SHAPE, G_SHAPE, jax.ShapeDtypeStru...  2.63 us
  transfers between devices with their start and end apart: 5, of which 2 were waited for; matrix products, arithmetic and copies ran while one was open for 0% of the time, Pallas kernels for 9%

profile of v2, /device:TPU:7, one launch (start us, length us, event | category | flops | bytes accessed | tf_op | source)
XLA Modules:
  0.0 70.5 jit_solution(7060647095939771251)
XLA Ops:
  0.6 0.0 copy-start.2
  0.6 0.0 copy-start.3
  0.7 0.0 copy-start.4
  0.7 1.8 %pack.1 = (f32[144,256]{1,0:T(8,128)}, f32[200,256]{1,0:T(8,128)}) custom-call(f32[256,256]{1,0:T(8,128)} %h_ref.3, f32[256,256]{1,0:T(8,128)} %c_ref.3), custom_call_target="tpu_custom_call" | custom-call | tf_op jit(solution)/shard_map/pack/pallas_call | solution.py:80
  2.5 1.3 %collective-permute-start.2 = (f32[200,256]{1,0:T(8,128)}, f32[200,256]{1,0:T(8,128)S(1)}, u32[]{:S(2)}, u32[]{:S(2)}) collective-permute-start(f32[200,256]{1,0:T(8,128)} %get-tuple-element.18), channel_id=1, source_target_pairs={{0,128},{64,192},{1,129},{65,193},{2,130},{66,194},{3,131},{67,195... | collective-permute-start | bytes 614408 | tf_op jit(solution)/shard_map/ppermute | solution.py:409
  3.8 1.3 %collective-permute-start = (f32[200,256]{1,0:T(8,128)}, f32[200,256]{1,0:T(8,128)S(1)}, u32[]{:S(2)}, u32[]{:S(2)}) collective-permute-start(f32[200,256]{1,0:T(8,128)} %get-tuple-element.18), channel_id=1, source_target_pairs={{0,64},{64,128},{128,192},{1,65},{65,129},{129,193},{2,66},{66,130... | collective-permute-start | bytes 614408 | tf_op jit(solution)/shard_map/ppermute | solution.py:410
  5.1 7.0 %collective-permute-done.2.mine_ref = f32[200,256]{1,0:T(8,128)S(1)} collective-permute-done((f32[200,256]{1,0:T(8,128)}, f32[200,256]{1,0:T(8,128)S(1)}, u32[]{:S(2)}, u32[]{:S(2)}) %collective-permute-start.2) | collective-permute-done | bytes 204832 | tf_op jit(solution)/shard_map/ppermute | solution.py:409
  12.1 1.5 %collective-permute-start.3 = (f32[200,256]{1,0:T(8,128)S(1)}, f32[200,256]{1,0:T(8,128)S(1)}, u32[]{:S(2)}, u32[]{:S(2)}) collective-permute-start(f32[200,256]{1,0:T(8,128)S(1)} %collective-permute-done.2.mine_ref), channel_id=1, source_target_pairs={{0,1},{1,0},{2,3},{3,2},{4,5},{5,4},{6,7},{7,6},{8,9},{9,8},{10,11... | collective-permute-start | bytes 614408 | tf_op jit(solution)/shard_map/ppermute | solution.py:411
  13.6 0.0 collective-permute-done.mine_ref
  13.6 0.0 collective-permute-start.1
  13.6 1.3 %collective-permute-start.4 = (f32[144,256]{1,0:T(8,128)}, f32[144,256]{1,0:T(8,128)S(1)}, u32[]{:S(2)}, u32[]{:S(2)}) collective-permute-start(f32[144,256]{1,0:T(8,128)} %get-tuple-element.19), channel_id=1, source_target_pairs={{0,192},{1,193},{2,194},{3,195},{4,196},{5,197},{6,198},{7,199},{8... | collective-permute-start | bytes 442376 | tf_op jit(solution)/shard_map/ppermute | solution.py:408
  16.2 0.0 copy-done.2
  16.2 0.0 copy-done.3
  16.2 0.0 copy-done.4
  16.2 2.8 %tables.1 = (s32[64,128]{1,0:T(8,128)S(1)}, s32[8,128]{1,0:T(8,128)S(1)}, s32[256,256]{1,0:T(8,128)S(1)}, s32[64,128]{1,0:T(8,128)S(1)}, s32[1]{0:T(128)}, /*index=5*/bf16[128,2304]{1,0:T(8,128)(2,1)S(1)}) custom-call(s32[32,256]{1,0:T(8,128)S(1)} %bitcast.5, s32[32,256]{1,0:T(8,128)S(1)} %bitcast.6, f32[2,6,64,64]{3,2,1,0:T(8,128)S(1)} %copy-done.2), custom_call_target="tpu_custom_call" | custom-call | tf_op jit(solution)/shard_map/tables/pallas_call | solution.py:296
  19.0 3.8 %collective-permute-done.4.head_ref = f32[144,256]{1,0:T(8,128)S(1)} collective-permute-done((f32[144,256]{1,0:T(8,128)}, f32[144,256]{1,0:T(8,128)S(1)}, u32[]{:S(2)}, u32[]{:S(2)}) %collective-permute-start.4) | collective-permute-done | bytes 147488 | tf_op jit(solution)/shard_map/ppermute | solution.py:408
  22.8 1.2 %first.1.g_in = f32[2,256,256]{2,1,0:T(8,128)S(1)} custom-call(f32[1]{0:T(128)S(6)} %copy.9.e_ref, f32[1]{0:T(128)S(6)} %copy.10.eta_ref, f32[144,256]{1,0:T(8,128)S(1)} %collective-permute-done.4.head_ref), custom_call_target="tpu_custom_call" | custom-call | tf_op jit(solution)/shard_map/first/pallas_call | solution.py:215
  24.0 0.0 collective-permute-done.3.other_ref
  24.0 2.1 %middle.2.g_in = f32[2,256,256]{2,1,0:T(8,128)S(1)} custom-call(f32[1]{0:T(128)S(6)} %copy.9.e_ref, f32[1]{0:T(128)S(6)} %copy.10.eta_ref, f32[200,256]{1,0:T(8,128)S(1)} %collective-permute-done.2.mine_ref, f32[200,256]{1,0:T(8,128)S(1)} %collective-permute-done.3.other_ref, f32[2,256,256]{2,1,0:T(8,128)S(1)} %first.1.g_in), custom_call_target="tpu_custom_call" | custom-call | tf_op jit(solution)/shard_map/middle/pallas_call | solution.py:227
  26.1 0.0 copy-start
  26.1 0.0 copy-start.1
  26.1 0.0 collective-permute-done.1.other_ref
  26.2 2.1 %middle.3.g_in = f32[2,256,256]{2,1,0:T(8,128)S(1)} custom-call(f32[1]{0:T(128)S(6)} %copy.9.e_ref, f32[1]{0:T(128)S(6)} %copy.10.eta_ref, f32[200,256]{1,0:T(8,128)S(1)} %collective-permute-done.mine_ref, f32[200,256]{1,0:T(8,128)S(1)} %collective-permute-done.1.other_ref, f32[2,256,256]{2,1,0:T(8,128)S(1)} %middle.2.g_in), custom_call_target="tpu_custom_call" | custom-call | tf_op jit(solution)/shard_map/middle/pallas_call | solution.py:227
  28.3 0.0 copy-done
  28.3 0.0 copy-done.1
  28.3 2.6 %last.1 = (f32[2,256,256]{2,1,0:T(8,128)S(1)}, f32[2,256,256]{2,1,0:T(8,128)S(1)}, f32[64,2,128]{2,1,0:T(2,128)S(1)}) custom-call(f32[1]{0:T(128)S(6)} %copy.9.e_ref, f32[1]{0:T(128)S(6)} %copy.10.eta_ref, f32[256,256]{1,0:T(8,128)S(1)} %copy-done, f32[256,256]{1,0:T(8,128)S(1)} %copy-done.1, f32[2,256,256]{2,1,0:T(8,128)S(1)} %middle.3.g_in, ...), custom_call_target="tpu_custom_call" | custom-call | tf_op jit(solution)/shard_map/last/pallas_call | solution.py:239
  31.0 22.1 %all_to_all.10.green_ref = f32[64,2,128]{2,1,0:T(2,128)S(1)} all-to-all(f32[64,2,128]{2,1,0:T(2,128)S(1)} %get-tuple-element.21), channel_id=1, replica_groups=mesh['slab'=4,'y'=4,'z'=8,'core'=2] {'y','z','core'}, dimensions={0} | all-to-all | bytes 131072 | tf_op jit(solution)/shard_map/all_to_all | solution.py:418
  53.0 0.3 convolve.1
  53.4 13.6 %all_to_all.11.self_ref = f32[64,2,128]{2,1,0:T(2,128)S(1)} all-to-all(f32[64,2,128]{2,1,0:T(2,128)S(1)} %convolve.1), channel_id=1, replica_groups=mesh['slab'=4,'y'=4,'z'=8,'core'=2] {'y','z','core'}, dimensions={0} | all-to-all | bytes 131072 | tf_op jit(solution)/shard_map/all_to_all | solution.py:420
  67.0 3.4 %correct.1 = (f32[1,2,256,256]{3,2,1,0:T(8,128)}, f32[64,2,128]{2,1,0:T(2,128)}) custom-call(s32[1]{0:T(128)} %get-tuple-element.15.rounds_ref, f32[64,2,128]{2,1,0:T(2,128)S(1)} %all_to_all.11.self_ref, s32[64,128]{1,0:T(8,128)S(1)} %get-tuple-element.22.next_ref, s32[256,256]{1,0:T(8,128)S(1)} %get-tuple-element.23.inverse_ref, ...), custom_call_target="tpu_custom_call" | custom-call | tf_op jit(solution)/shard_map/correct/pallas_call | solution.py:391
Async XLA Ops:
  0.6 15.6 %copy-start.2 = (f32[2,6,64,64]{3,2,1,0:T(8,128)S(1)}, f32[2,6,64,64]{3,2,1,0:T(8,128)}, u32[]{:S(2)}) copy-start(f32[2,6,64,64]{3,2,1,0:T(8,128)} %d_ref.1) | copy-start | bytes 589828
  0.6 15.6 %copy-start.3 = (s32[256,32]{0,1:T(8,128)S(1)}, s32[256,32]{0,1:T(8,128)}, u32[]{:S(2)}) copy-start(s32[256,32]{0,1:T(8,128)} %param.12) | copy-start | bytes 98308
  0.7 15.6 %copy-start.4 = (s32[256,32]{0,1:T(8,128)S(1)}, s32[256,32]{0,1:T(8,128)}, u32[]{:S(2)}) copy-start(s32[256,32]{0,1:T(8,128)} %param.13) | copy-start | bytes 98308
  2.5 9.6 %collective-permute-start.2 = (f32[200,256]{1,0:T(8,128)}, f32[200,256]{1,0:T(8,128)S(1)}, u32[]{:S(2)}, u32[]{:S(2)}) collective-permute-start(f32[200,256]{1,0:T(8,128)} %get-tuple-element.18), channel_id=1, source_target_pairs={{0,128},{64,192},{1,129},{65,193},{2,130},{66,194},{3,131},{67,195... | collective-permute-start | bytes 614408 | tf_op jit(solution)/shard_map/ppermute | solution.py:409
  3.8 9.8 %collective-permute-start = (f32[200,256]{1,0:T(8,128)}, f32[200,256]{1,0:T(8,128)S(1)}, u32[]{:S(2)}, u32[]{:S(2)}) collective-permute-start(f32[200,256]{1,0:T(8,128)} %get-tuple-element.18), channel_id=1, source_target_pairs={{0,64},{64,128},{128,192},{1,65},{65,129},{129,193},{2,66},{66,130... | collective-permute-start | bytes 614408 | tf_op jit(solution)/shard_map/ppermute | solution.py:410
  12.1 11.9 %collective-permute-start.3 = (f32[200,256]{1,0:T(8,128)S(1)}, f32[200,256]{1,0:T(8,128)S(1)}, u32[]{:S(2)}, u32[]{:S(2)}) collective-permute-start(f32[200,256]{1,0:T(8,128)S(1)} %collective-permute-done.2.mine_ref), channel_id=1, source_target_pairs={{0,1},{1,0},{2,3},{3,2},{4,5},{5,4},{6,7},{7,6},{8,9},{9,8},{10,11... | collective-permute-start | bytes 614408 | tf_op jit(solution)/shard_map/ppermute | solution.py:411
  13.6 12.5 %collective-permute-start.1 = (f32[200,256]{1,0:T(8,128)S(1)}, f32[200,256]{1,0:T(8,128)S(1)}, u32[]{:S(2)}, u32[]{:S(2)}) collective-permute-start(f32[200,256]{1,0:T(8,128)S(1)} %collective-permute-done.mine_ref), channel_id=1, source_target_pairs={{0,1},{1,0},{2,3},{3,2},{4,5},{5,4},{6,7},{7,6},{8,9},{9,8},{10,11... | collective-permute-start | bytes 614408 | tf_op jit(solution)/shard_map/ppermute | solution.py:412
  13.6 9.2 %collective-permute-start.4 = (f32[144,256]{1,0:T(8,128)}, f32[144,256]{1,0:T(8,128)S(1)}, u32[]{:S(2)}, u32[]{:S(2)}) collective-permute-start(f32[144,256]{1,0:T(8,128)} %get-tuple-element.19), channel_id=1, source_target_pairs={{0,192},{1,193},{2,194},{3,195},{4,196},{5,197},{6,198},{7,199},{8... | collective-permute-start | bytes 442376 | tf_op jit(solution)/shard_map/ppermute | solution.py:408
  26.1 2.2 %copy-start = (f32[256,256]{1,0:T(8,128)S(1)}, f32[256,256]{1,0:T(8,128)}, u32[]{:S(2)}) copy-start(f32[256,256]{1,0:T(8,128)} %h_ref.3) | copy-start | bytes 786436
  26.1 2.2 %copy-start.1 = (f32[256,256]{1,0:T(8,128)S(1)}, f32[256,256]{1,0:T(8,128)}, u32[]{:S(2)}) copy-start(f32[256,256]{1,0:T(8,128)} %c_ref.3) | copy-start | bytes 786436

commit v3 on v2

--- a/solution.py
+++ b/solution.py
@@ -23,6 +23,7 @@
 BF16 = jnp.bfloat16
 VMEM = pl.BlockSpec(memory_space=pltpu.VMEM)
 SMEM = pl.BlockSpec(memory_space=pltpu.SMEM)
+HBM = pl.BlockSpec(memory_space=pltpu.HBM)
 PARAMS = pltpu.CompilerParams(vmem_limit_bytes=16 * 1024 * 1024)
 
 
@@ -35,45 +36,75 @@
     return high, (x - high.astype(F32)).astype(BF16)
 
 
-def left_real(x):
-    high, low = split(x)
-    return jnp.concatenate([high, high, low], axis=1)
-
-
-def left_complex(real, imag):
-    return jnp.concatenate([left_real(real), left_real(imag)], axis=1)
-
-
-def right_real(real, imag):
-    real_high, real_low = split(real)
-    imag_high, imag_low = split(imag)
-    high = jnp.concatenate([real_high, imag_high], axis=1)
-    low = jnp.concatenate([real_low, imag_low], axis=1)
-    return jnp.concatenate([high, low, high], axis=0)
-
-
-def right_complex(real, imag):
-    return jnp.concatenate([right_real(real, imag), right_real(-imag, real)], axis=0)
-
-
-def product(left, right):
-    both = jnp.dot(left, right, preferred_element_type=F32)
-    return both[:, :B], both[:, B:]
-
-
-def pack_body(h_ref, c_ref, head_ref, piece_ref, payload):
+def dot(left, right):
+    return jnp.dot(left, right, preferred_element_type=F32)
+
+
+def dot_turned(left, right):
+    return lax.dot_general(left, right, (((1,), (1,)), ((), ())), preferred_element_type=F32)
+
+
+def stacked(real, imag):
+    high, low = split(jnp.concatenate([real, imag], axis=0))
+    return jnp.concatenate([high, low], axis=0)
+
+
+def three_passes(left, right_high, right_low, multiply=dot):
+    rows = left.shape[0] // 2
+    wide = multiply(left, right_high)
+    return wide[:rows] + wide[rows:] + multiply(left[:rows], right_low)
+
+
+def complex_product(left, right):
+    size = right.shape[0] // 4
+    by_real = three_passes(left, right[:size], right[2 * size : 3 * size])
+    by_imag = three_passes(left, right[size : 2 * size], right[3 * size :])
+    return by_real[:size] - by_imag[size:], by_real[size:] + by_imag[:size]
+
+
+def real_product(left, right):
+    size = right.shape[0] // 4
+    by_real = three_passes(left, right[:size], right[2 * size : 3 * size])
+    by_imag = three_passes(left, right[size : 2 * size], right[3 * size :])
+    return by_real, by_imag
+
+
+def pack_body(h_ref, c_ref, head_ref, piece_ref, h, sems):
+    core = lax.axis_index("core")
+    load = pltpu.make_async_copy(h_ref, h, sems.at[0])
+    load.start()
+    first_rows = PIECE - PACKED_H
+    begin = pltpu.make_async_copy(
+        c_ref.at[pl.ds(0, first_rows)], piece_ref.at[pl.ds(PACKED_H, first_rows)], sems.at[1]
+    )
+    rest = pltpu.make_async_copy(c_ref.at[pl.ds(first_rows, PIECE)], piece_ref, sems.at[1])
+
+    @pl.when(core == 0)
+    def _():
+        begin.start()
+
+    @pl.when(core != 0)
+    def _():
+        rest.start()
+
+    load.wait()
     row = iota((HALF, HALF), 0)
     col = iota((HALF, HALF), 1)
-    lower = h_ref[HALF:, HALF:]
-    payload[:HALF, :HALF] = jnp.where(row <= col, h_ref[:HALF, :HALF], lower)
-    payload[:HALF, HALF:] = h_ref[:HALF, HALF:]
+    lower = h[HALF:, HALF:]
+    head_ref[:HALF, :HALF] = jnp.where(row <= col, h[:HALF, :HALF], lower)
+    head_ref[:HALF, HALF:] = h[:HALF, HALF:]
     diagonal = jnp.sum(jnp.where(row == col, lower, 0.0), axis=0, keepdims=True)
-    payload[HALF:PACKED_H, :HALF] = jnp.broadcast_to(diagonal, (PACKED_H - HALF, HALF))
-    payload[HALF:PACKED_H, HALF:] = jnp.zeros((PACKED_H - HALF, HALF), F32)
-    payload[PACKED_H:, :] = c_ref[...]
-    head_ref[...] = payload[:PACKED_H, :]
-    start = pl.multiple_of(lax.axis_index("core") * PIECE, 8)
-    piece_ref[...] = payload[pl.ds(start, PIECE), :]
+    head_ref[HALF:PACKED_H, :HALF] = jnp.broadcast_to(diagonal, (PACKED_H - HALF, HALF))
+    head_ref[HALF:PACKED_H, HALF:] = jnp.zeros((PACKED_H - HALF, HALF), F32)
+
+    @pl.when(core == 0)
+    def _():
+        piece_ref[:PACKED_H, :] = head_ref[...]
+        begin.wait()
+
+    @pl.when(core != 0)
+    def _():
+        rest.wait()
 
 
 def pack(hamiltonian, coupling):
@@ -83,11 +114,12 @@
             jax.ShapeDtypeStruct((PACKED_H, B), F32),
             jax.ShapeDtypeStruct((PIECE, B), F32),
         ),
-        in_specs=[VMEM, VMEM],
+        in_specs=[HBM, HBM],
         out_specs=(VMEM, VMEM),
-        scratch_shapes=[pltpu.VMEM((PAYLOAD, B), F32)],
+        scratch_shapes=[pltpu.VMEM((B, B), F32), pltpu.SemaphoreType.DMA((2,))],
+        compiler_params=PARAMS,
         name="pack",
-    )(hamiltonian, coupling)
+    )(*(pltpu.with_memory_space_constraint(x, pltpu.HBM) for x in (hamiltonian, coupling)))
 
 
 def unpack_h(packed_ref, h):
@@ -133,15 +165,18 @@
         if negated_imag is None:
             z_real = outer_real * n_real
             z_imag = outer_imag * n_real
-            p_real, p_imag = product(left_real(n_real), right_real(z_real, z_imag))
+            high, low = split(n_real)
+            p_real, p_imag = real_product(
+                jnp.concatenate([high, low], axis=0), stacked(z_real, z_imag)
+            )
         else:
             n_imag = jnp.where(on, 0.0, -negated_imag)
             z_real = outer_real * n_real - outer_imag * n_imag
             z_imag = outer_real * n_imag + outer_imag * n_real
-            p_real, p_imag = product(left_complex(n_real, n_imag), right_complex(z_real, z_imag))
+            p_real, p_imag = complex_product(stacked(n_real, n_imag), stacked(z_real, z_imag))
         x_real = jnp.where(on, row_real, 0.0) - z_real
         x_imag = jnp.where(on, row_imag, 0.0) - z_imag
-        add_real, add_imag = product(left_complex(x_real, x_imag), right_complex(p_real, p_imag))
+        add_real, add_imag = complex_product(stacked(x_real, x_imag), stacked(p_real, p_imag))
         g_out[0] = x_real + add_real
         g_out[1] = x_imag + add_imag
         if p_out is not None:
@@ -157,11 +192,9 @@
         @pl.when(stage > 0)
         def _():
             c_high, c_low = split(c[...])
-            left = jnp.concatenate([c_high, c_high, c_low], axis=1)
-            t_real, t_imag = product(left, right_real(g_in[0], g_in[1]))
-            through = jnp.concatenate([left_real(t_real), left_real(t_imag)], axis=0)
-            right = jnp.concatenate([c_high, c_low, c_high], axis=1)
-            u = lax.dot_general(through, right, (((1,), (1,)), ((), ())), preferred_element_type=F32)
+            left = jnp.concatenate([c_high, c_low], axis=0)
+            t_real, t_imag = real_product(left, stacked(g_in[0], g_in[1]))
+            u = three_passes(stacked(t_real, t_imag), c_high, c_low, dot_turned)
             finish(h[...] + u[:B], u[B:])
 
 
@@ -275,7 +308,7 @@
         follower = jnp.where(same, lane + shift, follower)
         count = count + jnp.where(same, 1.0, 0.0)
     next_out[...] = follower
-    rounds_out[0] = jnp.max(count).astype(jnp.int32)
+    rounds_out[...] = jnp.broadcast_to(jnp.max(count, axis=0, keepdims=True), (8, 128))
     scale = 2.0 * math.sqrt(B / NEIGH)
     modes_count, energies = d_ref.shape[1], d_ref.shape[2]
     size = 2 * energies
@@ -300,11 +333,11 @@
             jax.ShapeDtypeStruct((8, 128), jnp.int32),
             jax.ShapeDtypeStruct((B, B), jnp.int32),
             jax.ShapeDtypeStruct((ROWS, 128), jnp.int32),
-            jax.ShapeDtypeStruct((1,), jnp.int32),
+            jax.ShapeDtypeStruct((8, 128), F32),
             jax.ShapeDtypeStruct((2 * energies, 6 * modes_count * energies), BF16),
         ),
         in_specs=[VMEM, VMEM, VMEM],
-        out_specs=(VMEM, VMEM, VMEM, VMEM, SMEM, VMEM),
+        out_specs=(VMEM, VMEM, VMEM, VMEM, VMEM, VMEM),
         scratch_shapes=[pltpu.VMEM((2, B, 128), jnp.int32)],
         compiler_params=PARAMS,
         name="tables",
@@ -337,7 +370,31 @@
     )(weight, mode, green)
 
 
-def correct_body(rounds_ref, self_ref, next_ref, inverse_ref, g_ref, p_ref, out_ref, self_out, moved):
+def beside_body(g_ref, p_ref, base_out, split_out):
+    g_stack = stacked(g_ref[0], g_ref[1])
+    split_out[...] = g_stack
+    p_stack = stacked(p_ref[0], p_ref[1])
+    square_real, square_imag = complex_product(p_stack, p_stack)
+    add_real, add_imag = complex_product(g_stack, stacked(square_real, square_imag))
+    base_out[0] = g_ref[0] + add_real
+    base_out[1] = g_ref[1] + add_imag
+
+
+def beside(g, p):
+    return pl.pallas_call(
+        beside_body,
+        out_shape=(G_SHAPE, jax.ShapeDtypeStruct((4 * B, B), BF16)),
+        in_specs=[VMEM, VMEM],
+        out_specs=(VMEM, VMEM),
+        compiler_params=PARAMS,
+        cost_estimate=pl.CostEstimate(
+            flops=2 * 24 * B * B * B, bytes_accessed=6 * 4 * B * B, transcendentals=0
+        ),
+        name="beside",
+    )(g, p)
+
+
+def correct_body(rounds_ref, self_ref, next_ref, inverse_ref, base_ref, split_ref, out_ref, self_out, moved):
     self_out[...] = self_ref[...]
     part_real = self_ref[:, 0, :]
     part_imag = self_ref[:, 1, :]
@@ -352,7 +409,7 @@
         return sum_real, sum_imag, jnp.where(valid, along_lanes(follower, index), -1)
 
     sum_real, sum_imag, _ = lax.fori_loop(
-        0, rounds_ref[0], gather_round, (part_real, part_imag, follower)
+        0, jnp.max(rounds_ref[...]).astype(jnp.int32), gather_round, (part_real, part_imag, follower)
     )
     reals, imags = [], []
     for q in range(GROUPS):
@@ -367,8 +424,8 @@
         imags.append(jnp.concatenate(row_imag, axis=1))
     sigma_real = jnp.concatenate(reals, axis=0)
     sigma_imag = jnp.concatenate(imags, axis=0)
-    g_real, g_imag = g_ref[0], g_ref[1]
-    s_real, s_imag = product(left_complex(sigma_real, sigma_imag), right_complex(g_real, g_imag))
+    g_stack = split_ref[...]
+    s_real, s_imag = complex_product(stacked(sigma_real, sigma_imag), g_stack)
     for q in range(GROUPS):
         rows = slice(q * ROWS, (q + 1) * ROWS)
         for part, value in enumerate((s_real, s_imag)):
@@ -377,37 +434,37 @@
                 moved[2 * part + side, pl.ds(q, ROWS, stride=GROUPS), :] = piece
     moved_real = jnp.concatenate([moved[0], moved[1]], axis=1)
     moved_imag = jnp.concatenate([moved[2], moved[3]], axis=1)
-    p_real, p_imag = p_ref[0], p_ref[1]
-    square_real, square_imag = product(left_complex(p_real, p_imag), right_complex(p_real, p_imag))
-    add_real, add_imag = product(
-        left_complex(g_real, g_imag),
-        right_complex(square_real + moved_real, square_imag + moved_imag),
-    )
-    out_ref[0, 0] = g_real + add_real
-    out_ref[0, 1] = g_imag + add_imag
-
-
-def correct(rounds, self_part, follower, inverse, g, p):
+    add_real, add_imag = complex_product(g_stack, stacked(moved_real, moved_imag))
+    out_ref[0, 0] = base_ref[0] + add_real
+    out_ref[0, 1] = base_ref[1] + add_imag
+
+
+def correct(rounds, self_part, follower, inverse, base, g_split):
     return pl.pallas_call(
         correct_body,
         out_shape=(
             jax.ShapeDtypeStruct((1, 2, B, B), F32),
             jax.ShapeDtypeStruct(self_part.shape, F32),
         ),
-        in_specs=[SMEM, VMEM, VMEM, VMEM, VMEM, VMEM],
+        in_specs=[VMEM] * 6,
         out_specs=(VMEM, VMEM),
         scratch_shapes=[pltpu.VMEM((4, B, HALF), F32)],
         compiler_params=PARAMS,
         name="correct",
-    )(rounds, self_part, follower, inverse, g, p)
+    )(rounds, self_part, follower, inverse, base, g_split)
+
+
+def shifted(x, distance):
+    count = lax.axis_size("slab")
+    return lax.ppermute(x, "slab", [(i, (i + distance) % count) for i in range(count)])
 
 
 def body(energies, broadening, hamiltonian, coupling, propagator, neighbors, phonon_modes):
     swap = [(0, 1), (1, 0)]
     head, piece = pack(hamiltonian, coupling)
-    head0 = lax.ppermute(head, "slab", [(0, 3)])
-    far = lax.ppermute(piece, "slab", [(0, 2), (1, 3)])
-    close = lax.ppermute(piece, "slab", [(0, 1), (1, 2), (2, 3)])
+    far = shifted(piece, 2)
+    head0 = shifted(head, 3)
+    close = shifted(piece, 1)
     far_other = lax.ppermute(far, "core", swap)
     close_other = lax.ppermute(close, "core", swap)
     near, mode, inverse, follower, rounds, weight = tables(neighbors.T, phonon_modes.T, propagator)
@@ -416,9 +473,10 @@
     g = middle(1, energies, broadening, close, close_other, g)
     g, p, pairs = last(energies, broadening, hamiltonian, coupling, g, near)
     regrouped = lax.all_to_all(pairs, ENERGY, 0, 0, tiled=True)
+    base, g_split = beside(g, p)
     owned = convolve(propagator.shape[1], weight, mode, regrouped)
     returned = lax.all_to_all(owned, ENERGY, 0, 0, tiled=True)
-    green, self_part = correct(rounds, returned, follower, inverse, g, p)
+    green, self_part = correct(rounds, returned, follower, inverse, base, g_split)
     self_part = jnp.swapaxes(self_part, 0, 1).reshape(1, 2, B * NEIGH)
     return green, self_part
 

time: 70.7 us -> 71 us (level)
  blocking collectives: 35.7 us -> 21.9 us
  starting transfers between devices: 5.39 us -> 12.9 us
  Pallas kernels: 16.5 us -> 19.9 us
  waiting for transfers between devices: 10.8 us -> 14 us
    all_to_all x1 -> x0, blocking collectives: 13.6 us -> none  [body(): returned = lax.all_to_all(owned, ENERGY, 0, 0, tiled=True)]
    all_to_all x0 -> x1, waiting for transfers between devices: none -> 7.98 us  [body(): returned = lax.all_to_all(owned, ENERGY, 0, 0, tiled=True)]
    ppermute x3, waiting for transfers between devices: 10.8 us -> 6.03 us  [shifted(): lax.ppermute(x, 'slab', [(i, (i + distance) % count) for i in range(count)])]
    all_to_all x0 -> x1, starting transfers between devices: none -> 4.44 us  [body(): returned = lax.all_to_all(owned, ENERGY, 0, 0, tiled=True)]
    pallas_call x0 -> x1, Pallas kernels: none -> 1.9 us  [beside(): pl.pallas_call(beside_body, out_shape=(G_SHAPE, jax.ShapeDtypeStruct((4 *...]
    ppermute x1, starting transfers between devices: 0.01 us -> 1.82 us  [body(): close_other = lax.ppermute(close, 'core', swap)]
    pallas_call x2, Pallas kernels: 4.28 us -> 5.84 us  [middle(): pl.pallas_call(functools.partial(middle_body, distance), out_shape=G_SHAP...]
    ppermute x3, starting transfers between devices: 3.85 us -> 5.13 us  [shifted(): lax.ppermute(x, 'slab', [(i, (i + distance) % count) for i in range(count)])]
  transfers between devices with their start and end apart: 5 -> 6, of which waited for: 2 -> 4; matrix products, arithmetic and copies ran while one was open for 0% -> 0% of each run, Pallas kernels for 9% -> 12%
where the time goes in v3:
time: 71 us; the launch traced here: 70.8 us
  blocking collectives  21.9 us (31%)
  Pallas kernels  19.9 us (28%)
  waiting for transfers between devices  14 us (20%)
  starting transfers between devices  12.9 us (18%)
  between operations  2.09 us (3%)
    all_to_all x1, blocking collectives, body(): regrouped = lax.all_to_all(pairs, ENERGY, 0, 0, tiled=True)  21.9 us
    all_to_all x1, waiting for transfers between devices, body(): returned = lax.all_to_all(owned, ENERGY, 0, 0, tiled=True)  7.98 us
    ppermute x3, waiting for transfers between devices, shifted(): lax.ppermute(x, 'slab', [(i, (i + distance) % count) for i in range(count)])  6.03 us
    pallas_call x2, Pallas kernels, middle(): pl.pallas_call(functools.partial(middle_body, distance), out_shape=G_SHAP...  5.84 us
    ppermute x3, starting transfers between devices, shifted(): lax.ppermute(x, 'slab', [(i, (i + distance) % count) for i in range(count)])  5.13 us
    all_to_all x1, starting transfers between devices, body(): returned = lax.all_to_all(owned, ENERGY, 0, 0, tiled=True)  4.44 us
    pallas_call x1, Pallas kernels, correct(): pl.pallas_call(correct_body, out_shape=(jax.ShapeDtypeStruct((1, 2, B, B)...  3.37 us
    pallas_call x1, Pallas kernels, last(): pl.pallas_call(last_body, out_shape=(G_SHAPE, G_SHAPE, jax.ShapeDtypeStru...  3.15 us
  transfers between devices with their start and end apart: 6, of which 4 were waited for; matrix products, arithmetic and copies ran while one was open for 0% of the time, Pallas kernels for 12%

profile of v3, /device:TPU:7, one launch (start us, length us, event | category | flops | bytes accessed | tf_op | source)
XLA Modules:
  0.0 70.8 jit_solution(6343017055546700685)
XLA Ops:
  0.6 0.0 copy-start.2
  0.6 0.0 copy-start.3
  0.7 0.0 copy-start.4
  0.7 1.1 %pack.1 = (f32[144,256]{1,0:T(8,128)S(1)}, f32[200,256]{1,0:T(8,128)S(1)}) custom-call(f32[256,256]{1,0:T(8,128)} %h_ref.3, f32[256,256]{1,0:T(8,128)} %c_ref.3), custom_call_target="tpu_custom_call" | custom-call | tf_op jit(solution)/shard_map/pack/pallas_call | solution.py:111
  1.7 1.2 %collective-permute-start.2 = (f32[200,256]{1,0:T(8,128)S(1)}, f32[200,256]{1,0:T(8,128)S(1)}, u32[]{:S(2)}, u32[]{:S(2)}) collective-permute-start(f32[200,256]{1,0:T(8,128)S(1)} %get-tuple-element.20), channel_id=1, source_target_pairs={{0,128},{64,192},{128,0},{192,64},{1,129},{65,193},{129,1},{193,65... | collective-permute-start | bytes 614408 | tf_op jit(solution)/shard_map/ppermute | solution.py:459
  3.0 1.8 %collective-permute-start = (f32[200,256]{1,0:T(8,128)S(1)}, f32[200,256]{1,0:T(8,128)S(1)}, u32[]{:S(2)}, u32[]{:S(2)}) collective-permute-start(f32[200,256]{1,0:T(8,128)S(1)} %get-tuple-element.20), channel_id=1, source_target_pairs={{0,64},{64,128},{128,192},{192,0},{1,65},{65,129},{129,193},{193,1... | collective-permute-start | bytes 614408 | tf_op jit(solution)/shard_map/ppermute | solution.py:459
  4.8 4.5 %collective-permute-done.2.mine_ref = f32[200,256]{1,0:T(8,128)S(1)} collective-permute-done((f32[200,256]{1,0:T(8,128)S(1)}, f32[200,256]{1,0:T(8,128)S(1)}, u32[]{:S(2)}, u32[]{:S(2)}) %collective-permute-start.2) | collective-permute-done | bytes 204832 | tf_op jit(solution)/shard_map/ppermute | solution.py:459
  9.3 1.5 %collective-permute-start.3 = (f32[200,256]{1,0:T(8,128)S(1)}, f32[200,256]{1,0:T(8,128)S(1)}, u32[]{:S(2)}, u32[]{:S(2)}) collective-permute-start(f32[200,256]{1,0:T(8,128)S(1)} %collective-permute-done.2.mine_ref), channel_id=1, source_target_pairs={{0,1},{1,0},{2,3},{3,2},{4,5},{5,4},{6,7},{7,6},{8,9},{9,8},{10,11... | collective-permute-start | bytes 614408 | tf_op jit(solution)/shard_map/ppermute | solution.py:468
  10.8 0.1 collective-permute-done.mine_ref
  11.0 1.8 %collective-permute-start.1 = (f32[200,256]{1,0:T(8,128)S(1)}, f32[200,256]{1,0:T(8,128)S(1)}, u32[]{:S(2)}, u32[]{:S(2)}) collective-permute-start(f32[200,256]{1,0:T(8,128)S(1)} %collective-permute-done.mine_ref), channel_id=1, source_target_pairs={{0,1},{1,0},{2,3},{3,2},{4,5},{5,4},{6,7},{7,6},{8,9},{9,8},{10,11... | collective-permute-start | bytes 614408 | tf_op jit(solution)/shard_map/ppermute | solution.py:469
  12.8 2.1 %collective-permute-start.4 = (f32[144,256]{1,0:T(8,128)S(1)}, f32[144,256]{1,0:T(8,128)S(1)}, u32[]{:S(2)}, u32[]{:S(2)}) collective-permute-start(f32[144,256]{1,0:T(8,128)S(1)} %get-tuple-element.21), channel_id=1, source_target_pairs={{0,192},{64,0},{128,64},{192,128},{1,193},{65,1},{129,65},{193,129... | collective-permute-start | bytes 442376 | tf_op jit(solution)/shard_map/ppermute | solution.py:459
  16.2 0.0 copy-done.2
  16.2 0.0 copy-done.3
  16.2 0.0 copy-done.4
  16.2 2.2 %tables.1 = (s32[64,128]{1,0:T(8,128)S(1)}, s32[8,128]{1,0:T(8,128)S(1)}, s32[256,256]{1,0:T(8,128)S(1)}, s32[64,128]{1,0:T(8,128)S(1)}, f32[8,128]{1,0:T(8,128)S(1)}, /*index=5*/bf16[128,2304]{1,0:T(8,128)(2,1)S(1)}) custom-call(s32[32,256]{1,0:T(8,128)S(1)} %bitcast.5, s32[32,256]{1,0:T(8,128)S(1)} %bitcast.6, f32[2,6,64,64]{3,2,1,0:T(8,128)S(1)} %copy-done.2), custom_call_target="tpu_custom_call" | custom-call | tf_op jit(solution)/shard_map/tables/pallas_call | solution.py:329
  18.5 1.3 %collective-permute-done.4.head_ref = f32[144,256]{1,0:T(8,128)S(1)} collective-permute-done((f32[144,256]{1,0:T(8,128)S(1)}, f32[144,256]{1,0:T(8,128)S(1)}, u32[]{:S(2)}, u32[]{:S(2)}) %collective-permute-start.4) | collective-permute-done | bytes 147488 | tf_op jit(solution)/shard_map/ppermute | solution.py:459
  19.8 1.3 %first.1.g_in = f32[2,256,256]{2,1,0:T(8,128)S(1)} custom-call(f32[1]{0:T(128)S(6)} %copy.9.e_ref, f32[1]{0:T(128)S(6)} %copy.10.eta_ref, f32[144,256]{1,0:T(8,128)S(1)} %collective-permute-done.4.head_ref), custom_call_target="tpu_custom_call" | custom-call | tf_op jit(solution)/shard_map/first/pallas_call | solution.py:248
  21.1 0.0 collective-permute-done.3.other_ref
  21.1 2.8 %middle.2.g_in = f32[2,256,256]{2,1,0:T(8,128)S(1)} custom-call(f32[1]{0:T(128)S(6)} %copy.9.e_ref, f32[1]{0:T(128)S(6)} %copy.10.eta_ref, f32[200,256]{1,0:T(8,128)S(1)} %collective-permute-done.2.mine_ref, f32[200,256]{1,0:T(8,128)S(1)} %collective-permute-done.3.other_ref, f32[2,256,256]{2,1,0:T(8,128)S(1)} %first.1.g_in), custom_call_target="tpu_custom_call" | custom-call | tf_op jit(solution)/shard_map/middle/pallas_call | solution.py:260
  24.0 0.0 copy-start
  24.0 0.0 copy-start.1
  24.0 0.0 collective-permute-done.1.other_ref
  24.0 3.0 %middle.3.g_in = f32[2,256,256]{2,1,0:T(8,128)S(1)} custom-call(f32[1]{0:T(128)S(6)} %copy.9.e_ref, f32[1]{0:T(128)S(6)} %copy.10.eta_ref, f32[200,256]{1,0:T(8,128)S(1)} %collective-permute-done.mine_ref, f32[200,256]{1,0:T(8,128)S(1)} %collective-permute-done.1.other_ref, f32[2,256,256]{2,1,0:T(8,128)S(1)} %middle.2.g_in), custom_call_target="tpu_custom_call" | custom-call | tf_op jit(solution)/shard_map/middle/pallas_call | solution.py:260
  27.0 0.0 copy-done
  27.0 0.0 copy-done.1
  27.0 3.1 %last.1 = (f32[2,256,256]{2,1,0:T(8,128)S(1)}, f32[2,256,256]{2,1,0:T(8,128)S(1)}, f32[64,2,128]{2,1,0:T(2,128)S(1)}) custom-call(f32[1]{0:T(128)S(6)} %copy.9.e_ref, f32[1]{0:T(128)S(6)} %copy.10.eta_ref, f32[256,256]{1,0:T(8,128)S(1)} %copy-done, f32[256,256]{1,0:T(8,128)S(1)} %copy-done.1, f32[2,256,256]{2,1,0:T(8,128)S(1)} %middle.3.g_in, ...), custom_call_target="tpu_custom_call" | custom-call | tf_op jit(solution)/shard_map/last/pallas_call | solution.py:272
  30.2 21.9 %all_to_all.10.green_ref = f32[64,2,128]{2,1,0:T(2,128)S(1)} all-to-all(f32[64,2,128]{2,1,0:T(2,128)S(1)} %get-tuple-element.23), channel_id=1, replica_groups=mesh['slab'=4,'y'=4,'z'=8,'core'=2] {'y','z','core'}, dimensions={0} | all-to-all | bytes 131072 | tf_op jit(solution)/shard_map/all_to_all | solution.py:475
  52.1 1.0 %convolve.1 = f32[64,2,128]{2,1,0:T(2,128)} custom-call(bf16[128,2304]{1,0:T(8,128)(2,1)S(1)} %get-tuple-element.18.weight_ref, s32[8,128]{1,0:T(8,128)S(1)} %get-tuple-element.19.mode_ref, f32[64,2,128]{2,1,0:T(2,128)S(1)} %all_to_all.10.green_ref), custom_call_target="tpu_custom_call" | custom-call | tf_op jit(solution)/shard_map/convolve/pallas_call | solution.py:363
  53.1 4.4 %all-to-all-start.1 = ((f32[64,2,128]{2,1,0:T(2,128)}), f32[64,2,128]{2,1,0:T(2,128)S(1)}, u32[]{:S(2)}, u32[]{:S(2)}) async-start(f32[64,2,128]{2,1,0:T(2,128)} %convolve.1), calls=%async_computation.1 | async-start | bytes 131072 | tf_op jit(solution)/shard_map/all_to_all | solution.py:478
  57.5 1.9 %beside.1 = (f32[2,256,256]{2,1,0:T(8,128)S(1)}, bf16[1024,256]{1,0:T(8,128)(2,1)S(1)}) custom-call(f32[2,256,256]{2,1,0:T(8,128)S(1)} %get-tuple-element.26.g_ref, f32[2,256,256]{2,1,0:T(8,128)S(1)} %get-tuple-element.27.p_ref), custom_call_target="tpu_custom_call" | custom-call | flops 805306368 | bytes 1572864 | tf_op jit(solution)/shard_map/beside/pallas_call | solution.py:384
  59.4 8.0 %all-to-all-done.1.self_ref = f32[64,2,128]{2,1,0:T(2,128)S(1)} async-done(((f32[64,2,128]{2,1,0:T(2,128)}), f32[64,2,128]{2,1,0:T(2,128)S(1)}, u32[]{:S(2)}, u32[]{:S(2)}) %all-to-all-start.1) | async-done | bytes 65568 | tf_op jit(solution)/shard_map/all_to_all | solution.py:478
  67.4 3.4 %correct.1 = (f32[1,2,256,256]{3,2,1,0:T(8,128)}, f32[64,2,128]{2,1,0:T(2,128)}) custom-call(f32[8,128]{1,0:T(8,128)S(1)} %get-tuple-element.17.rounds_ref, f32[64,2,128]{2,1,0:T(2,128)S(1)} %all-to-all-done.1.self_ref, s32[64,128]{1,0:T(8,128)S(1)} %get-tuple-element.24.next_ref, s32[256,256]{1,0:T(8,128)S(1)} %get-tuple-element.25.inverse_ref, ...), custom_call_target="tpu_custom_call" | custom-call | tf_op jit(solution)/shard_map/correct/pallas_call | solution.py:443
Async XLA Ops:
  0.6 15.6 %copy-start.2 = (f32[2,6,64,64]{3,2,1,0:T(8,128)S(1)}, f32[2,6,64,64]{3,2,1,0:T(8,128)}, u32[]{:S(2)}) copy-start(f32[2,6,64,64]{3,2,1,0:T(8,128)} %d_ref.1) | copy-start | bytes 589828
  0.6 15.6 %copy-start.3 = (s32[256,32]{0,1:T(8,128)S(1)}, s32[256,32]{0,1:T(8,128)}, u32[]{:S(2)}) copy-start(s32[256,32]{0,1:T(8,128)} %param.12) | copy-start | bytes 98308
  0.7 15.6 %copy-start.4 = (s32[256,32]{0,1:T(8,128)S(1)}, s32[256,32]{0,1:T(8,128)}, u32[]{:S(2)}) copy-start(s32[256,32]{0,1:T(8,128)} %param.13) | copy-start | bytes 98308
  1.7 7.6 %collective-permute-start.2 = (f32[200,256]{1,0:T(8,128)S(1)}, f32[200,256]{1,0:T(8,128)S(1)}, u32[]{:S(2)}, u32[]{:S(2)}) collective-permute-start(f32[200,256]{1,0:T(8,128)S(1)} %get-tuple-element.20), channel_id=1, source_target_pairs={{0,128},{64,192},{128,0},{192,64},{1,129},{65,193},{129,1},{193,65... | collective-permute-start | bytes 614408 | tf_op jit(solution)/shard_map/ppermute | solution.py:459
  3.0 8.0 %collective-permute-start = (f32[200,256]{1,0:T(8,128)S(1)}, f32[200,256]{1,0:T(8,128)S(1)}, u32[]{:S(2)}, u32[]{:S(2)}) collective-permute-start(f32[200,256]{1,0:T(8,128)S(1)} %get-tuple-element.20), channel_id=1, source_target_pairs={{0,64},{64,128},{128,192},{192,0},{1,65},{65,129},{129,193},{193,1... | collective-permute-start | bytes 614408 | tf_op jit(solution)/shard_map/ppermute | solution.py:459
  9.3 11.8 %collective-permute-start.3 = (f32[200,256]{1,0:T(8,128)S(1)}, f32[200,256]{1,0:T(8,128)S(1)}, u32[]{:S(2)}, u32[]{:S(2)}) collective-permute-start(f32[200,256]{1,0:T(8,128)S(1)} %collective-permute-done.2.mine_ref), channel_id=1, source_target_pairs={{0,1},{1,0},{2,3},{3,2},{4,5},{5,4},{6,7},{7,6},{8,9},{9,8},{10,11... | collective-permute-start | bytes 614408 | tf_op jit(solution)/shard_map/ppermute | solution.py:468
  11.0 13.0 %collective-permute-start.1 = (f32[200,256]{1,0:T(8,128)S(1)}, f32[200,256]{1,0:T(8,128)S(1)}, u32[]{:S(2)}, u32[]{:S(2)}) collective-permute-start(f32[200,256]{1,0:T(8,128)S(1)} %collective-permute-done.mine_ref), channel_id=1, source_target_pairs={{0,1},{1,0},{2,3},{3,2},{4,5},{5,4},{6,7},{7,6},{8,9},{9,8},{10,11... | collective-permute-start | bytes 614408 | tf_op jit(solution)/shard_map/ppermute | solution.py:469
  12.8 7.0 %collective-permute-start.4 = (f32[144,256]{1,0:T(8,128)S(1)}, f32[144,256]{1,0:T(8,128)S(1)}, u32[]{:S(2)}, u32[]{:S(2)}) collective-permute-start(f32[144,256]{1,0:T(8,128)S(1)} %get-tuple-element.21), channel_id=1, source_target_pairs={{0,192},{64,0},{128,64},{192,128},{1,193},{65,1},{129,65},{193,129... | collective-permute-start | bytes 442376 | tf_op jit(solution)/shard_map/ppermute | solution.py:459
  24.0 3.1 %copy-start = (f32[256,256]{1,0:T(8,128)S(1)}, f32[256,256]{1,0:T(8,128)}, u32[]{:S(2)}) copy-start(f32[256,256]{1,0:T(8,128)} %h_ref.3) | copy-start | bytes 786436
  24.0 3.1 %copy-start.1 = (f32[256,256]{1,0:T(8,128)S(1)}, f32[256,256]{1,0:T(8,128)}, u32[]{:S(2)}) copy-start(f32[256,256]{1,0:T(8,128)} %c_ref.3) | copy-start | bytes 786436
  53.1 14.3 %all-to-all-start.1 = ((f32[64,2,128]{2,1,0:T(2,128)}), f32[64,2,128]{2,1,0:T(2,128)S(1)}, u32[]{:S(2)}, u32[]{:S(2)}) async-start(f32[64,2,128]{2,1,0:T(2,128)} %convolve.1), calls=%async_computation.1 | async-start | bytes 131072 | tf_op jit(solution)/shard_map/all_to_all | solution.py:478

commit v4 on v3

--- a/solution.py
+++ b/solution.py
@@ -44,29 +44,18 @@
     return lax.dot_general(left, right, (((1,), (1,)), ((), ())), preferred_element_type=F32)
 
 
-def stacked(real, imag):
-    high, low = split(jnp.concatenate([real, imag], axis=0))
-    return jnp.concatenate([high, low], axis=0)
-
-
-def three_passes(left, right_high, right_low, multiply=dot):
-    rows = left.shape[0] // 2
-    wide = multiply(left, right_high)
-    return wide[:rows] + wide[rows:] + multiply(left[:rows], right_low)
+def three_passes(left, right, multiply=dot):
+    high, low = left
+    return multiply(high, right[0]) + multiply(low, right[0]) + multiply(high, right[1])
+
+
+def thirds(real, imag):
+    return split(real), split(imag), split(real + imag)
 
 
 def complex_product(left, right):
-    size = right.shape[0] // 4
-    by_real = three_passes(left, right[:size], right[2 * size : 3 * size])
-    by_imag = three_passes(left, right[size : 2 * size], right[3 * size :])
-    return by_real[:size] - by_imag[size:], by_real[size:] + by_imag[:size]
-
-
-def real_product(left, right):
-    size = right.shape[0] // 4
-    by_real = three_passes(left, right[:size], right[2 * size : 3 * size])
-    by_imag = three_passes(left, right[size : 2 * size], right[3 * size :])
-    return by_real, by_imag
+    first, second, mixed = (three_passes(x, y) for x, y in zip(left, right))
+    return first - second, mixed - first - second
 
 
 def pack_body(h_ref, c_ref, head_ref, piece_ref, h, sems):
@@ -165,18 +154,16 @@
         if negated_imag is None:
             z_real = outer_real * n_real
             z_imag = outer_imag * n_real
-            high, low = split(n_real)
-            p_real, p_imag = real_product(
-                jnp.concatenate([high, low], axis=0), stacked(z_real, z_imag)
-            )
+            n_split = split(n_real)
+            p_real, p_imag = (three_passes(n_split, split(z)) for z in (z_real, z_imag))
         else:
             n_imag = jnp.where(on, 0.0, -negated_imag)
             z_real = outer_real * n_real - outer_imag * n_imag
             z_imag = outer_real * n_imag + outer_imag * n_real
-            p_real, p_imag = complex_product(stacked(n_real, n_imag), stacked(z_real, z_imag))
+            p_real, p_imag = complex_product(thirds(n_real, n_imag), thirds(z_real, z_imag))
         x_real = jnp.where(on, row_real, 0.0) - z_real
         x_imag = jnp.where(on, row_imag, 0.0) - z_imag
-        add_real, add_imag = complex_product(stacked(x_real, x_imag), stacked(p_real, p_imag))
+        add_real, add_imag = complex_product(thirds(x_real, x_imag), thirds(p_real, p_imag))
         g_out[0] = x_real + add_real
         g_out[1] = x_imag + add_imag
         if p_out is not None:
@@ -191,11 +178,12 @@
 
         @pl.when(stage > 0)
         def _():
-            c_high, c_low = split(c[...])
-            left = jnp.concatenate([c_high, c_low], axis=0)
-            t_real, t_imag = real_product(left, stacked(g_in[0], g_in[1]))
-            u = three_passes(stacked(t_real, t_imag), c_high, c_low, dot_turned)
-            finish(h[...] + u[:B], u[B:])
+            c_split = split(c[...])
+            u_real, u_imag = (
+                three_passes(split(three_passes(c_split, split(g_in[part]))), c_split, dot_turned)
+                for part in range(2)
+            )
+            finish(h[...] + u_real, u_imag)
 
 
 def first_body(e_ref, eta_ref, head_ref, g_out, h):
@@ -370,32 +358,11 @@
     )(weight, mode, green)
 
 
-def beside_body(g_ref, p_ref, base_out, split_out):
-    g_stack = stacked(g_ref[0], g_ref[1])
-    split_out[...] = g_stack
-    p_stack = stacked(p_ref[0], p_ref[1])
-    square_real, square_imag = complex_product(p_stack, p_stack)
-    add_real, add_imag = complex_product(g_stack, stacked(square_real, square_imag))
-    base_out[0] = g_ref[0] + add_real
-    base_out[1] = g_ref[1] + add_imag
-
-
-def beside(g, p):
-    return pl.pallas_call(
-        beside_body,
-        out_shape=(G_SHAPE, jax.ShapeDtypeStruct((4 * B, B), BF16)),
-        in_specs=[VMEM, VMEM],
-        out_specs=(VMEM, VMEM),
-        compiler_params=PARAMS,
-        cost_estimate=pl.CostEstimate(
-            flops=2 * 24 * B * B * B, bytes_accessed=6 * 4 * B * B, transcendentals=0
-        ),
-        name="beside",
-    )(g, p)
-
-
-def correct_body(rounds_ref, self_ref, next_ref, inverse_ref, base_ref, split_ref, out_ref, self_out, moved):
-    self_out[...] = self_ref[...]
+def correct_body(
+    rounds_ref, self_ref, next_ref, inverse_ref, g_ref, p_ref, out_ref, self_out, moved, result, sems
+):
+    pass_on = pltpu.make_async_copy(self_ref, self_out, sems.at[0])
+    pass_on.start()
     part_real = self_ref[:, 0, :]
     part_imag = self_ref[:, 1, :]
     follower = next_ref[...]
@@ -424,8 +391,8 @@
         imags.append(jnp.concatenate(row_imag, axis=1))
     sigma_real = jnp.concatenate(reals, axis=0)
     sigma_imag = jnp.concatenate(imags, axis=0)
-    g_stack = split_ref[...]
-    s_real, s_imag = complex_product(stacked(sigma_real, sigma_imag), g_stack)
+    g_real, g_imag = g_ref[0], g_ref[1]
+    s_real, s_imag = complex_product(thirds(sigma_real, sigma_imag), thirds(g_real, g_imag))
     for q in range(GROUPS):
         rows = slice(q * ROWS, (q + 1) * ROWS)
         for part, value in enumerate((s_real, s_imag)):
@@ -434,12 +401,24 @@
                 moved[2 * part + side, pl.ds(q, ROWS, stride=GROUPS), :] = piece
     moved_real = jnp.concatenate([moved[0], moved[1]], axis=1)
     moved_imag = jnp.concatenate([moved[2], moved[3]], axis=1)
-    add_real, add_imag = complex_product(g_stack, stacked(moved_real, moved_imag))
-    out_ref[0, 0] = base_ref[0] + add_real
-    out_ref[0, 1] = base_ref[1] + add_imag
-
-
-def correct(rounds, self_part, follower, inverse, base, g_split):
+    p_thirds = thirds(p_ref[0], p_ref[1])
+    square_real, square_imag = complex_product(p_thirds, p_thirds)
+    right = thirds(square_real + moved_real, square_imag + moved_imag)
+    leaving = []
+    for half in range(2):
+        rows = slice(half * HALF, (half + 1) * HALF)
+        add_real, add_imag = complex_product(thirds(g_real[rows], g_imag[rows]), right)
+        result[0, rows, :] = g_real[rows] + add_real
+        result[1, rows, :] = g_imag[rows] + add_imag
+        out = pltpu.make_async_copy(result.at[:, rows, :], out_ref.at[0, :, rows, :], sems.at[1 + half])
+        out.start()
+        leaving.append(out)
+    pass_on.wait()
+    for out in leaving:
+        out.wait()
+
+
+def correct(rounds, self_part, follower, inverse, g, p):
     return pl.pallas_call(
         correct_body,
         out_shape=(
@@ -447,11 +426,15 @@
             jax.ShapeDtypeStruct(self_part.shape, F32),
         ),
         in_specs=[VMEM] * 6,
-        out_specs=(VMEM, VMEM),
-        scratch_shapes=[pltpu.VMEM((4, B, HALF), F32)],
+        out_specs=(HBM, HBM),
+        scratch_shapes=[
+            pltpu.VMEM((4, B, HALF), F32),
+            pltpu.VMEM((2, B, B), F32),
+            pltpu.SemaphoreType.DMA((3,)),
+        ],
         compiler_params=PARAMS,
         name="correct",
-    )(rounds, self_part, follower, inverse, base, g_split)
+    )(rounds, self_part, follower, inverse, g, p)
 
 
 def shifted(x, distance):
@@ -473,10 +456,9 @@
     g = middle(1, energies, broadening, close, close_other, g)
     g, p, pairs = last(energies, broadening, hamiltonian, coupling, g, near)
     regrouped = lax.all_to_all(pairs, ENERGY, 0, 0, tiled=True)
-    base, g_split = beside(g, p)
     owned = convolve(propagator.shape[1], weight, mode, regrouped)
     returned = lax.all_to_all(owned, ENERGY, 0, 0, tiled=True)
-    green, self_part = correct(rounds, returned, follower, inverse, base, g_split)
+    green, self_part = correct(rounds, returned, follower, inverse, g, p)
     self_part = jnp.swapaxes(self_part, 0, 1).reshape(1, 2, B * NEIGH)
     return green, self_part
 

time: 71 us -> 66.7 us (0.939)
  blocking collectives: 21.9 us -> 35.5 us
  waiting for transfers between devices: 14 us -> 6.04 us
  Pallas kernels: 19.9 us -> 14.2 us
  starting transfers between devices: 12.9 us -> 8.46 us
    all_to_all x0 -> x1, blocking collectives: none -> 13.6 us  [body(): returned = lax.all_to_all(owned, ENERGY, 0, 0, tiled=True)]
    all_to_all x1 -> x0, waiting for transfers between devices: 7.98 us -> none  [body(): returned = lax.all_to_all(owned, ENERGY, 0, 0, tiled=True)]
    all_to_all x1 -> x0, starting transfers between devices: 4.44 us -> none  [body(): returned = lax.all_to_all(owned, ENERGY, 0, 0, tiled=True)]
    pallas_call x1 -> x0, Pallas kernels: 1.9 us -> none  [beside(): pl.pallas_call(beside_body, out_shape=(G_SHAPE, jax.ShapeDtypeStruct((4 *...]
    pallas_call x2, Pallas kernels: 5.84 us -> 4.15 us  [middle(): pl.pallas_call(functools.partial(middle_body, distance), out_shape=G_SHAP...]
  transfers between devices with their start and end apart: 6 -> 5, of which waited for: 4 -> 3; matrix products, arithmetic and copies ran while one was open for 0% -> 0% of each run, Pallas kernels for 12% -> 8%
where the time goes in v4:
time: 66.7 us; the launch traced here: 66.5 us
  blocking collectives  35.5 us (53%)
  Pallas kernels  14.2 us (21%)
  starting transfers between devices  8.46 us (13%)
  waiting for transfers between devices  6.04 us (9%)
  between operations  2.24 us (3%)
    all_to_all x1, blocking collectives, body(): regrouped = lax.all_to_all(pairs, ENERGY, 0, 0, tiled=True)  21.9 us
    all_to_all x1, blocking collectives, body(): returned = lax.all_to_all(owned, ENERGY, 0, 0, tiled=True)  13.6 us
    ppermute x3, waiting for transfers between devices, shifted(): lax.ppermute(x, 'slab', [(i, (i + distance) % count) for i in range(count)])  6.03 us
    ppermute x3, starting transfers between devices, shifted(): lax.ppermute(x, 'slab', [(i, (i + distance) % count) for i in range(count)])  5.13 us
    pallas_call x2, Pallas kernels, middle(): pl.pallas_call(functools.partial(middle_body, distance), out_shape=G_SHAP...  4.15 us
    pallas_call x1, Pallas kernels, correct(): pl.pallas_call(correct_body, out_shape=(jax.ShapeDtypeStruct((1, 2, B, B)...  2.73 us
    pallas_call x1, Pallas kernels, last(): pl.pallas_call(last_body, out_shape=(G_SHAPE, G_SHAPE, jax.ShapeDtypeStru...  2.59 us
    pallas_call x1, Pallas kernels, tables(): pl.pallas_call(tables_body, out_shape=(jax.ShapeDtypeStruct((ROWS, 128),...  2.23 us
  transfers between devices with their start and end apart: 5, of which 3 were waited for; matrix products, arithmetic and copies ran while one was open for 0% of the time, Pallas kernels for 8%

profile of v4, /device:TPU:7, one launch (start us, length us, event | category | flops | bytes accessed | tf_op | source)
XLA Modules:
  0.0 66.5 jit_solution(6701551253818356612)
XLA Ops:
  0.6 0.0 copy-start.2
  0.6 0.0 copy-start.3
  0.7 0.0 copy-start.4
  0.7 1.1 %pack.1 = (f32[144,256]{1,0:T(8,128)S(1)}, f32[200,256]{1,0:T(8,128)S(1)}) custom-call(f32[256,256]{1,0:T(8,128)} %h_ref.3, f32[256,256]{1,0:T(8,128)} %c_ref.3), custom_call_target="tpu_custom_call" | custom-call | tf_op jit(solution)/shard_map/pack/pallas_call | solution.py:100
  1.7 1.2 %collective-permute-start.2 = (f32[200,256]{1,0:T(8,128)S(1)}, f32[200,256]{1,0:T(8,128)S(1)}, u32[]{:S(2)}, u32[]{:S(2)}) collective-permute-start(f32[200,256]{1,0:T(8,128)S(1)} %get-tuple-element.18), channel_id=1, source_target_pairs={{0,128},{64,192},{128,0},{192,64},{1,129},{65,193},{129,1},{193,65... | collective-permute-start | bytes 614408 | tf_op jit(solution)/shard_map/ppermute | solution.py:442
  3.0 1.8 %collective-permute-start = (f32[200,256]{1,0:T(8,128)S(1)}, f32[200,256]{1,0:T(8,128)S(1)}, u32[]{:S(2)}, u32[]{:S(2)}) collective-permute-start(f32[200,256]{1,0:T(8,128)S(1)} %get-tuple-element.18), channel_id=1, source_target_pairs={{0,64},{64,128},{128,192},{192,0},{1,65},{65,129},{129,193},{193,1... | collective-permute-start | bytes 614408 | tf_op jit(solution)/shard_map/ppermute | solution.py:442
  4.8 4.5 %collective-permute-done.2.mine_ref = f32[200,256]{1,0:T(8,128)S(1)} collective-permute-done((f32[200,256]{1,0:T(8,128)S(1)}, f32[200,256]{1,0:T(8,128)S(1)}, u32[]{:S(2)}, u32[]{:S(2)}) %collective-permute-start.2) | collective-permute-done | bytes 204832 | tf_op jit(solution)/shard_map/ppermute | solution.py:442
  9.3 1.5 %collective-permute-start.3 = (f32[200,256]{1,0:T(8,128)S(1)}, f32[200,256]{1,0:T(8,128)S(1)}, u32[]{:S(2)}, u32[]{:S(2)}) collective-permute-start(f32[200,256]{1,0:T(8,128)S(1)} %collective-permute-done.2.mine_ref), channel_id=1, source_target_pairs={{0,1},{1,0},{2,3},{3,2},{4,5},{5,4},{6,7},{7,6},{8,9},{9,8},{10,11... | collective-permute-start | bytes 614408 | tf_op jit(solution)/shard_map/ppermute | solution.py:451
  10.8 0.1 collective-permute-done.mine_ref
  11.0 1.8 %collective-permute-start.1 = (f32[200,256]{1,0:T(8,128)S(1)}, f32[200,256]{1,0:T(8,128)S(1)}, u32[]{:S(2)}, u32[]{:S(2)}) collective-permute-start(f32[200,256]{1,0:T(8,128)S(1)} %collective-permute-done.mine_ref), channel_id=1, source_target_pairs={{0,1},{1,0},{2,3},{3,2},{4,5},{5,4},{6,7},{7,6},{8,9},{9,8},{10,11... | collective-permute-start | bytes 614408 | tf_op jit(solution)/shard_map/ppermute | solution.py:452
  12.8 2.1 %collective-permute-start.4 = (f32[144,256]{1,0:T(8,128)S(1)}, f32[144,256]{1,0:T(8,128)S(1)}, u32[]{:S(2)}, u32[]{:S(2)}) collective-permute-start(f32[144,256]{1,0:T(8,128)S(1)} %get-tuple-element.19), channel_id=1, source_target_pairs={{0,192},{64,0},{128,64},{192,128},{1,193},{65,1},{129,65},{193,129... | collective-permute-start | bytes 442376 | tf_op jit(solution)/shard_map/ppermute | solution.py:442
  16.2 0.0 copy-done.2
  16.2 0.0 copy-done.3
  16.2 0.0 copy-done.4
  16.2 2.2 %tables.1 = (s32[64,128]{1,0:T(8,128)S(1)}, s32[8,128]{1,0:T(8,128)S(1)}, s32[256,256]{1,0:T(8,128)S(1)}, s32[64,128]{1,0:T(8,128)S(1)}, f32[8,128]{1,0:T(8,128)S(1)}, /*index=5*/bf16[128,2304]{1,0:T(8,128)(2,1)S(1)}) custom-call(s32[32,256]{1,0:T(8,128)S(1)} %bitcast.5, s32[32,256]{1,0:T(8,128)S(1)} %bitcast.6, f32[2,6,64,64]{3,2,1,0:T(8,128)S(1)} %copy-done.2), custom_call_target="tpu_custom_call" | custom-call | tf_op jit(solution)/shard_map/tables/pallas_call | solution.py:317
  18.5 1.3 %collective-permute-done.4.head_ref = f32[144,256]{1,0:T(8,128)S(1)} collective-permute-done((f32[144,256]{1,0:T(8,128)S(1)}, f32[144,256]{1,0:T(8,128)S(1)}, u32[]{:S(2)}, u32[]{:S(2)}) %collective-permute-start.4) | collective-permute-done | bytes 147488 | tf_op jit(solution)/shard_map/ppermute | solution.py:442
  19.8 1.1 %first.1.g_in = f32[2,256,256]{2,1,0:T(8,128)S(1)} custom-call(f32[1]{0:T(128)S(6)} %copy.9.e_ref, f32[1]{0:T(128)S(6)} %copy.10.eta_ref, f32[144,256]{1,0:T(8,128)S(1)} %collective-permute-done.4.head_ref), custom_call_target="tpu_custom_call" | custom-call | tf_op jit(solution)/shard_map/first/pallas_call | solution.py:236
  20.9 0.0 collective-permute-done.3.other_ref
  20.9 2.1 %middle.2.g_in = f32[2,256,256]{2,1,0:T(8,128)S(1)} custom-call(f32[1]{0:T(128)S(6)} %copy.9.e_ref, f32[1]{0:T(128)S(6)} %copy.10.eta_ref, f32[200,256]{1,0:T(8,128)S(1)} %collective-permute-done.2.mine_ref, f32[200,256]{1,0:T(8,128)S(1)} %collective-permute-done.3.other_ref, f32[2,256,256]{2,1,0:T(8,128)S(1)} %first.1.g_in), custom_call_target="tpu_custom_call" | custom-call | tf_op jit(solution)/shard_map/middle/pallas_call | solution.py:248
  23.0 0.0 copy-start
  23.0 0.0 copy-start.1
  23.0 0.0 collective-permute-done.1.other_ref
  23.0 2.1 %middle.3.g_in = f32[2,256,256]{2,1,0:T(8,128)S(1)} custom-call(f32[1]{0:T(128)S(6)} %copy.9.e_ref, f32[1]{0:T(128)S(6)} %copy.10.eta_ref, f32[200,256]{1,0:T(8,128)S(1)} %collective-permute-done.mine_ref, f32[200,256]{1,0:T(8,128)S(1)} %collective-permute-done.1.other_ref, f32[2,256,256]{2,1,0:T(8,128)S(1)} %middle.2.g_in), custom_call_target="tpu_custom_call" | custom-call | tf_op jit(solution)/shard_map/middle/pallas_call | solution.py:248
  25.1 0.0 copy-done
  25.1 0.0 copy-done.1
  25.1 2.6 %last.1 = (f32[2,256,256]{2,1,0:T(8,128)S(1)}, f32[2,256,256]{2,1,0:T(8,128)S(1)}, f32[64,2,128]{2,1,0:T(2,128)S(1)}) custom-call(f32[1]{0:T(128)S(6)} %copy.9.e_ref, f32[1]{0:T(128)S(6)} %copy.10.eta_ref, f32[256,256]{1,0:T(8,128)S(1)} %copy-done, f32[256,256]{1,0:T(8,128)S(1)} %copy-done.1, f32[2,256,256]{2,1,0:T(8,128)S(1)} %middle.3.g_in, ...), custom_call_target="tpu_custom_call" | custom-call | tf_op jit(solution)/shard_map/last/pallas_call | solution.py:260
  27.7 21.9 %all_to_all.10.green_ref = f32[64,2,128]{2,1,0:T(2,128)S(1)} all-to-all(f32[64,2,128]{2,1,0:T(2,128)S(1)} %get-tuple-element.21), channel_id=1, replica_groups=mesh['slab'=4,'y'=4,'z'=8,'core'=2] {'y','z','core'}, dimensions={0} | all-to-all | bytes 131072 | tf_op jit(solution)/shard_map/all_to_all | solution.py:458
  49.6 0.3 convolve.1
  50.0 13.6 %all_to_all.11.self_ref = f32[64,2,128]{2,1,0:T(2,128)S(1)} all-to-all(f32[64,2,128]{2,1,0:T(2,128)S(1)} %convolve.1), channel_id=1, replica_groups=mesh['slab'=4,'y'=4,'z'=8,'core'=2] {'y','z','core'}, dimensions={0} | all-to-all | bytes 131072 | tf_op jit(solution)/shard_map/all_to_all | solution.py:460
  63.6 2.7 %correct.1 = (f32[1,2,256,256]{3,2,1,0:T(8,128)}, f32[64,2,128]{2,1,0:T(2,128)}) custom-call(f32[8,128]{1,0:T(8,128)S(1)} %get-tuple-element.15.rounds_ref, f32[64,2,128]{2,1,0:T(2,128)S(1)} %all_to_all.11.self_ref, s32[64,128]{1,0:T(8,128)S(1)} %get-tuple-element.22.next_ref, s32[256,256]{1,0:T(8,128)S(1)} %get-tuple-element.23.inverse_ref, ...), custom_call_target="tpu_custom_call" | custom-call | tf_op jit(solution)/shard_map/correct/pallas_call | solution.py:422
Async XLA Ops:
  0.6 15.6 %copy-start.2 = (f32[2,6,64,64]{3,2,1,0:T(8,128)S(1)}, f32[2,6,64,64]{3,2,1,0:T(8,128)}, u32[]{:S(2)}) copy-start(f32[2,6,64,64]{3,2,1,0:T(8,128)} %d_ref.1) | copy-start | bytes 589828
  0.6 15.6 %copy-start.3 = (s32[256,32]{0,1:T(8,128)S(1)}, s32[256,32]{0,1:T(8,128)}, u32[]{:S(2)}) copy-start(s32[256,32]{0,1:T(8,128)} %param.12) | copy-start | bytes 98308
  0.7 15.6 %copy-start.4 = (s32[256,32]{0,1:T(8,128)S(1)}, s32[256,32]{0,1:T(8,128)}, u32[]{:S(2)}) copy-start(s32[256,32]{0,1:T(8,128)} %param.13) | copy-start | bytes 98308
  1.7 7.6 %collective-permute-start.2 = (f32[200,256]{1,0:T(8,128)S(1)}, f32[200,256]{1,0:T(8,128)S(1)}, u32[]{:S(2)}, u32[]{:S(2)}) collective-permute-start(f32[200,256]{1,0:T(8,128)S(1)} %get-tuple-element.18), channel_id=1, source_target_pairs={{0,128},{64,192},{128,0},{192,64},{1,129},{65,193},{129,1},{193,65... | collective-permute-start | bytes 614408 | tf_op jit(solution)/shard_map/ppermute | solution.py:442
  3.0 8.0 %collective-permute-start = (f32[200,256]{1,0:T(8,128)S(1)}, f32[200,256]{1,0:T(8,128)S(1)}, u32[]{:S(2)}, u32[]{:S(2)}) collective-permute-start(f32[200,256]{1,0:T(8,128)S(1)} %get-tuple-element.18), channel_id=1, source_target_pairs={{0,64},{64,128},{128,192},{192,0},{1,65},{65,129},{129,193},{193,1... | collective-permute-start | bytes 614408 | tf_op jit(solution)/shard_map/ppermute | solution.py:442
  9.3 11.6 %collective-permute-start.3 = (f32[200,256]{1,0:T(8,128)S(1)}, f32[200,256]{1,0:T(8,128)S(1)}, u32[]{:S(2)}, u32[]{:S(2)}) collective-permute-start(f32[200,256]{1,0:T(8,128)S(1)} %collective-permute-done.2.mine_ref), channel_id=1, source_target_pairs={{0,1},{1,0},{2,3},{3,2},{4,5},{5,4},{6,7},{7,6},{8,9},{9,8},{10,11... | collective-permute-start | bytes 614408 | tf_op jit(solution)/shard_map/ppermute | solution.py:451
  11.0 12.0 %collective-permute-start.1 = (f32[200,256]{1,0:T(8,128)S(1)}, f32[200,256]{1,0:T(8,128)S(1)}, u32[]{:S(2)}, u32[]{:S(2)}) collective-permute-start(f32[200,256]{1,0:T(8,128)S(1)} %collective-permute-done.mine_ref), channel_id=1, source_target_pairs={{0,1},{1,0},{2,3},{3,2},{4,5},{5,4},{6,7},{7,6},{8,9},{9,8},{10,11... | collective-permute-start | bytes 614408 | tf_op jit(solution)/shard_map/ppermute | solution.py:452
  12.8 7.0 %collective-permute-start.4 = (f32[144,256]{1,0:T(8,128)S(1)}, f32[144,256]{1,0:T(8,128)S(1)}, u32[]{:S(2)}, u32[]{:S(2)}) collective-permute-start(f32[144,256]{1,0:T(8,128)S(1)} %get-tuple-element.19), channel_id=1, source_target_pairs={{0,192},{64,0},{128,64},{192,128},{1,193},{65,1},{129,65},{193,129... | collective-permute-start | bytes 442376 | tf_op jit(solution)/shard_map/ppermute | solution.py:442
  23.0 2.1 %copy-start = (f32[256,256]{1,0:T(8,128)S(1)}, f32[256,256]{1,0:T(8,128)}, u32[]{:S(2)}) copy-start(f32[256,256]{1,0:T(8,128)} %h_ref.3) | copy-start | bytes 786436
  23.0 2.1 %copy-start.1 = (f32[256,256]{1,0:T(8,128)S(1)}, f32[256,256]{1,0:T(8,128)}, u32[]{:S(2)}) copy-start(f32[256,256]{1,0:T(8,128)} %c_ref.3) | copy-start | bytes 786436

commit v5 on v4

--- a/solution.py
+++ b/solution.py
@@ -17,7 +17,9 @@
 PACKED_H = HALF + 16
 PAYLOAD = PACKED_H + B
 PIECE = PAYLOAD // 2
+HEAD = PACKED_H // 2
 GROUPS = 4
+CHAIN = 3
 ROWS = B // GROUPS
 F32 = jnp.float32
 BF16 = jnp.bfloat16
@@ -58,7 +60,7 @@
     return first - second, mixed - first - second
 
 
-def pack_body(h_ref, c_ref, head_ref, piece_ref, h, sems):
+def pack_body(h_ref, c_ref, head_out, piece_ref, h, head_ref, sems):
     core = lax.axis_index("core")
     load = pltpu.make_async_copy(h_ref, h, sems.at[0])
     load.start()
@@ -89,10 +91,12 @@
     @pl.when(core == 0)
     def _():
         piece_ref[:PACKED_H, :] = head_ref[...]
+        head_out[...] = head_ref[:HEAD, :]
         begin.wait()
 
     @pl.when(core != 0)
     def _():
+        head_out[...] = head_ref[HEAD:, :]
         rest.wait()
 
 
@@ -100,12 +104,16 @@
     return pl.pallas_call(
         pack_body,
         out_shape=(
-            jax.ShapeDtypeStruct((PACKED_H, B), F32),
+            jax.ShapeDtypeStruct((HEAD, B), F32),
             jax.ShapeDtypeStruct((PIECE, B), F32),
         ),
         in_specs=[HBM, HBM],
         out_specs=(VMEM, VMEM),
-        scratch_shapes=[pltpu.VMEM((B, B), F32), pltpu.SemaphoreType.DMA((2,))],
+        scratch_shapes=[
+            pltpu.VMEM((B, B), F32),
+            pltpu.VMEM((PACKED_H, B), F32),
+            pltpu.SemaphoreType.DMA((2,)),
+        ],
         compiler_params=PARAMS,
         name="pack",
     )(*(pltpu.with_memory_space_constraint(x, pltpu.HBM) for x in (hamiltonian, coupling)))
@@ -186,12 +194,20 @@
             finish(h[...] + u_real, u_imag)
 
 
-def first_body(e_ref, eta_ref, head_ref, g_out, h):
+def join(mine_ref, other_ref, whole):
+    core = lax.axis_index("core")
+    rows = mine_ref.shape[0]
+    whole[pl.ds(pl.multiple_of(core * rows, 8), rows), :] = mine_ref[...]
+    whole[pl.ds(pl.multiple_of((1 - core) * rows, 8), rows), :] = other_ref[...]
+
+
+def first_body(e_ref, eta_ref, mine_ref, other_ref, g_out, packed, h):
     stage = lax.axis_index("slab") - 3
 
     @pl.when(stage >= 0)
     def _():
-        unpack_h(head_ref, h)
+        join(mine_ref, other_ref, packed)
+        unpack_h(packed, h)
         stage_math(stage, e_ref, eta_ref, h, None, None, g_out, None)
 
 
@@ -200,9 +216,7 @@
 
     @pl.when(stage >= 0)
     def _():
-        core = lax.axis_index("core")
-        payload[pl.ds(pl.multiple_of(core * PIECE, 8), PIECE), :] = mine_ref[...]
-        payload[pl.ds(pl.multiple_of((1 - core) * PIECE, 8), PIECE), :] = other_ref[...]
+        join(mine_ref, other_ref, payload)
         unpack_h(payload, h)
         stage_math(stage, e_ref, eta_ref, h, payload.at[PACKED_H:, :], g_in, g_out, None)
 
@@ -211,19 +225,19 @@
     return jnp.take_along_axis(x, index, axis=1)
 
 
-def last_body(e_ref, eta_ref, h_ref, c_ref, g_in, near_ref, g_out, p_out, pair_out, halves):
+def last_body(e_ref, eta_ref, _, h_ref, c_ref, g_in, near_ref, g_out, p_out, pair_out, halves):
     stage_math(lax.axis_index("slab"), e_ref, eta_ref, h_ref, c_ref, g_in, g_out, p_out)
     near = near_ref[...]
     inside = jnp.bitwise_and(near, HALF - 1)
     upper = near >= HALF
     group = iota((ROWS, 128), 1) // NEIGH
     for part in range(2):
-        halves[0] = g_out[part, :, :HALF]
-        halves[1] = g_out[part, :, HALF:]
+        halves[2 * part] = g_out[part, :, :HALF]
+        halves[2 * part + 1] = g_out[part, :, HALF:]
         result = jnp.zeros((ROWS, 128), F32)
         for q in range(GROUPS):
-            left = halves[0, pl.ds(q, ROWS, stride=GROUPS), :]
-            right = halves[1, pl.ds(q, ROWS, stride=GROUPS), :]
+            left = halves[2 * part, pl.ds(q, ROWS, stride=GROUPS), :]
+            right = halves[2 * part + 1, pl.ds(q, ROWS, stride=GROUPS), :]
             picked = jnp.where(upper, along_lanes(right, inside), along_lanes(left, inside))
             result = jnp.where(group == q, picked, result)
         pair_out[:, part, :] = result
@@ -232,16 +246,16 @@
 G_SHAPE = jax.ShapeDtypeStruct((2, B, B), F32)
 
 
-def first(e, eta, head):
+def first(e, eta, mine, other):
     return pl.pallas_call(
         first_body,
         out_shape=G_SHAPE,
-        in_specs=[SMEM, SMEM, VMEM],
+        in_specs=[SMEM, SMEM, VMEM, VMEM],
         out_specs=VMEM,
-        scratch_shapes=[pltpu.VMEM((B, B), F32)],
+        scratch_shapes=[pltpu.VMEM((PACKED_H, B), F32), pltpu.VMEM((B, B), F32)],
         compiler_params=PARAMS,
         name="first",
-    )(e, eta, head)
+    )(e, eta, mine, other)
 
 
 def middle(distance, e, eta, mine, other, g):
@@ -256,16 +270,16 @@
     )(e, eta, mine, other, g)
 
 
-def last(e, eta, hamiltonian, coupling, g, near):
+def last(e, eta, rounds, hamiltonian, coupling, g, near):
     return pl.pallas_call(
         last_body,
         out_shape=(G_SHAPE, G_SHAPE, jax.ShapeDtypeStruct((ROWS, 2, 128), F32)),
-        in_specs=[SMEM, SMEM, VMEM, VMEM, VMEM, VMEM],
+        in_specs=[SMEM, SMEM, SMEM, VMEM, VMEM, VMEM, VMEM],
         out_specs=(VMEM, VMEM, VMEM),
-        scratch_shapes=[pltpu.VMEM((2, B, HALF), F32)],
+        scratch_shapes=[pltpu.VMEM((4, B, HALF), F32)],
         compiler_params=PARAMS,
         name="last",
-    )(e, eta, hamiltonian, coupling, g, near)
+    )(e, eta, rounds, hamiltonian, coupling, g, near)
 
 
 def tables_body(near_ref, mode_ref, d_ref, near_out, mode_out, inverse_out, next_out, rounds_out, weight_out, wide):
@@ -295,7 +309,11 @@
         same = (pltpu.roll(near, 128 - shift, axis=1) == near) & (place + shift < NEIGH)
         follower = jnp.where(same, lane + shift, follower)
         count = count + jnp.where(same, 1.0, 0.0)
-    next_out[...] = follower
+    chain = follower
+    for step in range(CHAIN):
+        next_out[step] = chain
+        beyond = along_lanes(follower, jnp.maximum(chain, 0))
+        chain = jnp.where(chain >= 0, beyond, -1)
     rounds_out[...] = jnp.broadcast_to(jnp.max(count, axis=0, keepdims=True), (8, 128))
     scale = 2.0 * math.sqrt(B / NEIGH)
     modes_count, energies = d_ref.shape[1], d_ref.shape[2]
@@ -320,7 +338,7 @@
             jax.ShapeDtypeStruct((ROWS, 128), jnp.int32),
             jax.ShapeDtypeStruct((8, 128), jnp.int32),
             jax.ShapeDtypeStruct((B, B), jnp.int32),
-            jax.ShapeDtypeStruct((ROWS, 128), jnp.int32),
+            jax.ShapeDtypeStruct((CHAIN, ROWS, 128), jnp.int32),
             jax.ShapeDtypeStruct((8, 128), F32),
             jax.ShapeDtypeStruct((2 * energies, 6 * modes_count * energies), BF16),
         ),
@@ -365,18 +383,25 @@
     pass_on.start()
     part_real = self_ref[:, 0, :]
     part_imag = self_ref[:, 1, :]
-    follower = next_ref[...]
-
-    def gather_round(_, carry):
-        sum_real, sum_imag, pointer = carry
+
+    def gather_round(sum_real, sum_imag, pointer):
         valid = pointer >= 0
         index = jnp.maximum(pointer, 0)
         sum_real = sum_real + jnp.where(valid, along_lanes(part_real, index), 0.0)
         sum_imag = sum_imag + jnp.where(valid, along_lanes(part_imag, index), 0.0)
-        return sum_real, sum_imag, jnp.where(valid, along_lanes(follower, index), -1)
-
+        return sum_real, sum_imag
+
+    def later_round(_, carry):
+        sum_real, sum_imag, pointer = carry
+        beyond = along_lanes(next_ref[0], jnp.maximum(pointer, 0))
+        pointer = jnp.where(pointer >= 0, beyond, -1)
+        return *gather_round(sum_real, sum_imag, pointer), pointer
+
+    sum_real, sum_imag = part_real, part_imag
+    for step in range(CHAIN):
+        sum_real, sum_imag = gather_round(sum_real, sum_imag, next_ref[step])
     sum_real, sum_imag, _ = lax.fori_loop(
-        0, jnp.max(rounds_ref[...]).astype(jnp.int32), gather_round, (part_real, part_imag, follower)
+        CHAIN, rounds_ref[0], later_round, (sum_real, sum_imag, next_ref[CHAIN - 1])
     )
     reals, imags = [], []
     for q in range(GROUPS):
@@ -404,18 +429,18 @@
     p_thirds = thirds(p_ref[0], p_ref[1])
     square_real, square_imag = complex_product(p_thirds, p_thirds)
     right = thirds(square_real + moved_real, square_imag + moved_imag)
-    leaving = []
-    for half in range(2):
-        rows = slice(half * HALF, (half + 1) * HALF)
-        add_real, add_imag = complex_product(thirds(g_real[rows], g_imag[rows]), right)
-        result[0, rows, :] = g_real[rows] + add_real
-        result[1, rows, :] = g_imag[rows] + add_imag
-        out = pltpu.make_async_copy(result.at[:, rows, :], out_ref.at[0, :, rows, :], sems.at[1 + half])
-        out.start()
-        leaving.append(out)
+    left = thirds(g_real, g_imag)
+    first = three_passes(left[0], right[0])
+    second = three_passes(left[1], right[1])
+    result[0] = g_real + (first - second)
+    leave_real = pltpu.make_async_copy(result.at[0], out_ref.at[0, 0], sems.at[1])
+    leave_real.start()
+    result[1] = g_imag + (three_passes(left[2], right[2]) - first - second)
+    leave_imag = pltpu.make_async_copy(result.at[1], out_ref.at[0, 1], sems.at[2])
+    leave_imag.start()
     pass_on.wait()
-    for out in leaving:
-        out.wait()
+    leave_real.wait()
+    leave_imag.wait()
 
 
 def correct(rounds, self_part, follower, inverse, g, p):
@@ -425,7 +450,7 @@
             jax.ShapeDtypeStruct((1, 2, B, B), F32),
             jax.ShapeDtypeStruct(self_part.shape, F32),
         ),
-        in_specs=[VMEM] * 6,
+        in_specs=[SMEM] + [VMEM] * 5,
         out_specs=(HBM, HBM),
         scratch_shapes=[
             pltpu.VMEM((4, B, HALF), F32),
@@ -445,16 +470,18 @@
 def body(energies, broadening, hamiltonian, coupling, propagator, neighbors, phonon_modes):
     swap = [(0, 1), (1, 0)]
     head, piece = pack(hamiltonian, coupling)
-    far = shifted(piece, 2)
+    far = lax.ppermute(piece, "slab", [(0, 2), (1, 3), (2, 1), (3, 0)])
     head0 = shifted(head, 3)
     close = shifted(piece, 1)
     far_other = lax.ppermute(far, "core", swap)
+    head_other = lax.ppermute(head0, "core", swap)
     close_other = lax.ppermute(close, "core", swap)
     near, mode, inverse, follower, rounds, weight = tables(neighbors.T, phonon_modes.T, propagator)
-    g = first(energies, broadening, head0)
+    rounds = jnp.max(rounds[:1]).astype(jnp.int32).reshape(1)
+    g = first(energies, broadening, head0, head_other)
     g = middle(2, energies, broadening, far, far_other, g)
     g = middle(1, energies, broadening, close, close_other, g)
-    g, p, pairs = last(energies, broadening, hamiltonian, coupling, g, near)
+    g, p, pairs = last(energies, broadening, rounds, hamiltonian, coupling, g, near)
     regrouped = lax.all_to_all(pairs, ENERGY, 0, 0, tiled=True)
     owned = convolve(propagator.shape[1], weight, mode, regrouped)
     returned = lax.all_to_all(owned, ENERGY, 0, 0, tiled=True)

time: 66.7 us -> 66.5 us (level)
  waiting for transfers between devices: 6.04 us -> 4.55 us
  between operations: 2.24 us -> 2.92 us
    ppermute x3 -> x2, waiting for transfers between devices: 6.03 us -> 0.01 us  [shifted(): lax.ppermute(x, 'slab', [(i, (i + distance) % count) for i in range(count)])]
    ppermute x0 -> x2, waiting for transfers between devices: none -> 4.54 us  [the longest x1 4.54 us: body(): far = lax.ppermute(piece, 'slab', [(0, 2), (1, 3), (2, 1), (3, 0)])]
    ppermute x3 -> x2, starting transfers between devices: 5.13 us -> 5.57 us  [shifted(): lax.ppermute(x, 'slab', [(i, (i + distance) % count) for i in range(count)])]
  transfers between devices with their start and end apart: 5 -> 6, of which waited for: 3 -> 1; matrix products, arithmetic and copies ran while one was open for 0% -> 1% of each run, Pallas kernels for 8% -> 8%
where the time goes in v5:
time: 66.5 us; the launch traced here: 66.3 us
  blocking collectives  35 us (53%)
  Pallas kernels  14.2 us (21%)
  starting transfers between devices  8.96 us (13%)
  waiting for transfers between devices  4.55 us (7%)
  between operations  2.92 us (4%)
    all_to_all x1, blocking collectives, body(): regrouped = lax.all_to_all(pairs, ENERGY, 0, 0, tiled=True)  21.4 us
    all_to_all x1, blocking collectives, body(): returned = lax.all_to_all(owned, ENERGY, 0, 0, tiled=True)  13.6 us
    ppermute x2, starting transfers between devices, shifted(): lax.ppermute(x, 'slab', [(i, (i + distance) % count) for i in range(count)])  5.57 us
    ppermute x1, waiting for transfers between devices, body(): far = lax.ppermute(piece, 'slab', [(0, 2), (1, 3), (2, 1), (3, 0)])  4.54 us
    pallas_call x2, Pallas kernels, middle(): pl.pallas_call(functools.partial(middle_body, distance), out_shape=G_SHAP...  4.34 us
    pallas_call x1, Pallas kernels, correct(): pl.pallas_call(correct_body, out_shape=(jax.ShapeDtypeStruct((1, 2, B, B)...  2.52 us
    pallas_call x1, Pallas kernels, last(): pl.pallas_call(last_body, out_shape=(G_SHAPE, G_SHAPE, jax.ShapeDtypeStru...  2.41 us
    pallas_call x1, Pallas kernels, tables(): pl.pallas_call(tables_body, out_shape=(jax.ShapeDtypeStruct((ROWS, 128),...  2.38 us
  transfers between devices with their start and end apart: 6, of which 1 were waited for; matrix products, arithmetic and copies ran while one was open for 1% of the time, Pallas kernels for 8%

profile of v5, /device:TPU:7, one launch (start us, length us, event | category | flops | bytes accessed | tf_op | source)
XLA Modules:
  0.0 66.3 jit_solution(13869869661771828131)
XLA Ops:
  0.6 0.0 copy-start.2
  0.6 0.0 copy-start.3
  0.7 0.0 copy-start.4
  0.7 1.1 %pack.1 = (f32[72,256]{1,0:T(8,128)S(1)}, f32[200,256]{1,0:T(8,128)S(1)}) custom-call(f32[256,256]{1,0:T(8,128)} %h_ref.3, f32[256,256]{1,0:T(8,128)} %c_ref.3), custom_call_target="tpu_custom_call" | custom-call | tf_op jit(solution)/shard_map/pack/pallas_call | solution.py:104
  1.7 0.1 collective-permute-start.2
  1.8 2.9 %collective-permute-start = (f32[200,256]{1,0:T(8,128)S(1)}, f32[200,256]{1,0:T(8,128)S(1)}, u32[]{:S(2)}, u32[]{:S(2)}) collective-permute-start(f32[200,256]{1,0:T(8,128)S(1)} %get-tuple-element.18), channel_id=1, source_target_pairs={{0,64},{64,128},{128,192},{192,0},{1,65},{65,129},{129,193},{193,1... | collective-permute-start | bytes 614408 | tf_op jit(solution)/shard_map/ppermute | solution.py:467
  4.8 4.5 %collective-permute-done.2.mine_ref = f32[200,256]{1,0:T(8,128)S(1)} collective-permute-done((f32[200,256]{1,0:T(8,128)S(1)}, f32[200,256]{1,0:T(8,128)S(1)}, u32[]{:S(2)}, u32[]{:S(2)}) %collective-permute-start.2) | collective-permute-done | bytes 204832 | tf_op jit(solution)/shard_map/ppermute | solution.py:473
  9.3 1.5 %collective-permute-start.3 = (f32[200,256]{1,0:T(8,128)S(1)}, f32[200,256]{1,0:T(8,128)S(1)}, u32[]{:S(2)}, u32[]{:S(2)}) collective-permute-start(f32[200,256]{1,0:T(8,128)S(1)} %collective-permute-done.2.mine_ref), channel_id=1, source_target_pairs={{0,1},{1,0},{2,3},{3,2},{4,5},{5,4},{6,7},{7,6},{8,9},{9,8},{10,11... | collective-permute-start | bytes 614408 | tf_op jit(solution)/shard_map/ppermute | solution.py:476
  10.8 0.0 collective-permute-done.mine_ref
  10.8 1.4 %collective-permute-start.1 = (f32[200,256]{1,0:T(8,128)S(1)}, f32[200,256]{1,0:T(8,128)S(1)}, u32[]{:S(2)}, u32[]{:S(2)}) collective-permute-start(f32[200,256]{1,0:T(8,128)S(1)} %collective-permute-done.mine_ref), channel_id=1, source_target_pairs={{0,1},{1,0},{2,3},{3,2},{4,5},{5,4},{6,7},{7,6},{8,9},{9,8},{10,11... | collective-permute-start | bytes 614408 | tf_op jit(solution)/shard_map/ppermute | solution.py:478
  12.2 2.6 %collective-permute-start.4 = (f32[72,256]{1,0:T(8,128)S(1)}, f32[72,256]{1,0:T(8,128)S(1)}, u32[]{:S(2)}, u32[]{:S(2)}) collective-permute-start(f32[72,256]{1,0:T(8,128)S(1)} %get-tuple-element.19), channel_id=1, source_target_pairs={{0,192},{64,0},{128,64},{192,128},{1,193},{65,1},{129,65},{193,129... | collective-permute-start | bytes 221192 | tf_op jit(solution)/shard_map/ppermute | solution.py:467
  16.2 0.0 copy-done.2
  16.2 0.0 copy-done.3
  16.2 0.0 copy-done.4
  16.2 2.4 %tables.1 = (s32[64,128]{1,0:T(8,128)S(1)}, s32[8,128]{1,0:T(8,128)S(1)}, s32[256,256]{1,0:T(8,128)S(1)}, s32[3,64,128]{2,1,0:T(8,128)S(1)}, f32[8,128]{1,0:T(8,128)S(1)}, /*index=5*/bf16[128,2304]{1,0:T(8,128)(2,1)S(1)}) custom-call(s32[32,256]{1,0:T(8,128)S(1)} %bitcast.6, s32[32,256]{1,0:T(8,128)S(1)} %bitcast.7, f32[2,6,64,64]{3,2,1,0:T(8,128)S(1)} %copy-done.2), custom_call_target="tpu_custom_call" | custom-call | tf_op jit(solution)/shard_map/tables/pallas_call | solution.py:335
  18.6 0.0 collective-permute-done.4.mine_ref
  18.6 0.4 collective-permute-start.5
  19.0 0.6 slice_reduce_fusion
  20.2 0.0 collective-permute-done.5.other_ref
  20.2 1.1 %first.1.g_in = f32[2,256,256]{2,1,0:T(8,128)S(1)} custom-call(f32[1]{0:T(128)S(6)} %copy.9.e_ref, f32[1]{0:T(128)S(6)} %copy.10.eta_ref, f32[72,256]{1,0:T(8,128)S(1)} %collective-permute-done.4.mine_ref, f32[72,256]{1,0:T(8,128)S(1)} %collective-permute-done.5.other_ref), custom_call_target="tpu_custom_call" | custom-call | tf_op jit(solution)/shard_map/first/pallas_call | solution.py:250
  21.4 0.0 collective-permute-done.3.other_ref
  21.4 2.1 %middle.2.g_in = f32[2,256,256]{2,1,0:T(8,128)S(1)} custom-call(f32[1]{0:T(128)S(6)} %copy.9.e_ref, f32[1]{0:T(128)S(6)} %copy.10.eta_ref, f32[200,256]{1,0:T(8,128)S(1)} %collective-permute-done.2.mine_ref, f32[200,256]{1,0:T(8,128)S(1)} %collective-permute-done.3.other_ref, f32[2,256,256]{2,1,0:T(8,128)S(1)} %first.1.g_in), custom_call_target="tpu_custom_call" | custom-call | tf_op jit(solution)/shard_map/middle/pallas_call | solution.py:262
  23.5 0.0 copy-start
  23.5 0.0 copy-start.1
  23.5 0.0 collective-permute-done.1.other_ref
  23.5 2.3 %middle.3.g_in = f32[2,256,256]{2,1,0:T(8,128)S(1)} custom-call(f32[1]{0:T(128)S(6)} %copy.9.e_ref, f32[1]{0:T(128)S(6)} %copy.10.eta_ref, f32[200,256]{1,0:T(8,128)S(1)} %collective-permute-done.mine_ref, f32[200,256]{1,0:T(8,128)S(1)} %collective-permute-done.1.other_ref, f32[2,256,256]{2,1,0:T(8,128)S(1)} %middle.2.g_in), custom_call_target="tpu_custom_call" | custom-call | tf_op jit(solution)/shard_map/middle/pallas_call | solution.py:262
  25.8 0.0 copy-done
  25.8 0.0 copy-done.1
  25.8 2.4 %last.1 = (f32[2,256,256]{2,1,0:T(8,128)S(1)}, f32[2,256,256]{2,1,0:T(8,128)S(1)}, f32[64,2,128]{2,1,0:T(2,128)S(1)}) custom-call(f32[1]{0:T(128)S(6)} %copy.9.e_ref, f32[1]{0:T(128)S(6)} %copy.10.eta_ref, s32[1]{0:T(128)} %bitcast.2._.rounds_ref, f32[256,256]{1,0:T(8,128)S(1)} %copy-done, f32[256,256]{1,0:T(8,128)S(1)} %copy-done.1, ...), custom_call_target="tpu_custom_call" | custom-call | tf_op jit(solution)/shard_map/last/pallas_call | solution.py:274
  28.2 21.4 %all_to_all.10.green_ref = f32[64,2,128]{2,1,0:T(2,128)S(1)} all-to-all(f32[64,2,128]{2,1,0:T(2,128)S(1)} %get-tuple-element.21), channel_id=1, replica_groups=mesh['slab'=4,'y'=4,'z'=8,'core'=2] {'y','z','core'}, dimensions={0} | all-to-all | bytes 131072 | tf_op jit(solution)/shard_map/all_to_all | solution.py:485
  49.6 0.3 convolve.1
  50.0 13.6 %all_to_all.11.self_ref = f32[64,2,128]{2,1,0:T(2,128)S(1)} all-to-all(f32[64,2,128]{2,1,0:T(2,128)S(1)} %convolve.1), channel_id=1, replica_groups=mesh['slab'=4,'y'=4,'z'=8,'core'=2] {'y','z','core'}, dimensions={0} | all-to-all | bytes 131072 | tf_op jit(solution)/shard_map/all_to_all | solution.py:487
  63.6 2.5 %correct.1 = (f32[1,2,256,256]{3,2,1,0:T(8,128)}, f32[64,2,128]{2,1,0:T(2,128)}) custom-call(s32[1]{0:T(128)} %bitcast.2._.rounds_ref, f32[64,2,128]{2,1,0:T(2,128)S(1)} %all_to_all.11.self_ref, s32[3,64,128]{2,1,0:T(8,128)S(1)} %get-tuple-element.22.next_ref, s32[256,256]{1,0:T(8,128)S(1)} %get-tuple-element.23.inverse_ref, ...), custom_call_target="tpu_custom_call" | custom-call | tf_op jit(solution)/shard_map/correct/pallas_call | solution.py:447
Async XLA Ops:
  0.6 15.6 %copy-start.2 = (f32[2,6,64,64]{3,2,1,0:T(8,128)S(1)}, f32[2,6,64,64]{3,2,1,0:T(8,128)}, u32[]{:S(2)}) copy-start(f32[2,6,64,64]{3,2,1,0:T(8,128)} %d_ref.1) | copy-start | bytes 589828
  0.6 15.6 %copy-start.3 = (s32[256,32]{0,1:T(8,128)S(1)}, s32[256,32]{0,1:T(8,128)}, u32[]{:S(2)}) copy-start(s32[256,32]{0,1:T(8,128)} %param.12) | copy-start | bytes 98308
  0.7 15.6 %copy-start.4 = (s32[256,32]{0,1:T(8,128)S(1)}, s32[256,32]{0,1:T(8,128)}, u32[]{:S(2)}) copy-start(s32[256,32]{0,1:T(8,128)} %param.13) | copy-start | bytes 98308
  1.7 7.6 %collective-permute-start.2 = (f32[200,256]{1,0:T(8,128)S(1)}, f32[200,256]{1,0:T(8,128)S(1)}, u32[]{:S(2)}, u32[]{:S(2)}) collective-permute-start(f32[200,256]{1,0:T(8,128)S(1)} %get-tuple-element.18), channel_id=1, source_target_pairs={{0,128},{64,192},{128,64},{192,0},{1,129},{65,193},{129,65},{193,1... | collective-permute-start | bytes 614408 | tf_op jit(solution)/shard_map/ppermute | solution.py:473
  1.8 9.0 %collective-permute-start = (f32[200,256]{1,0:T(8,128)S(1)}, f32[200,256]{1,0:T(8,128)S(1)}, u32[]{:S(2)}, u32[]{:S(2)}) collective-permute-start(f32[200,256]{1,0:T(8,128)S(1)} %get-tuple-element.18), channel_id=1, source_target_pairs={{0,64},{64,128},{128,192},{192,0},{1,65},{65,129},{129,193},{193,1... | collective-permute-start | bytes 614408 | tf_op jit(solution)/shard_map/ppermute | solution.py:467
  9.3 12.1 %collective-permute-start.3 = (f32[200,256]{1,0:T(8,128)S(1)}, f32[200,256]{1,0:T(8,128)S(1)}, u32[]{:S(2)}, u32[]{:S(2)}) collective-permute-start(f32[200,256]{1,0:T(8,128)S(1)} %collective-permute-done.2.mine_ref), channel_id=1, source_target_pairs={{0,1},{1,0},{2,3},{3,2},{4,5},{5,4},{6,7},{7,6},{8,9},{9,8},{10,11... | collective-permute-start | bytes 614408 | tf_op jit(solution)/shard_map/ppermute | solution.py:476
  10.8 12.7 %collective-permute-start.1 = (f32[200,256]{1,0:T(8,128)S(1)}, f32[200,256]{1,0:T(8,128)S(1)}, u32[]{:S(2)}, u32[]{:S(2)}) collective-permute-start(f32[200,256]{1,0:T(8,128)S(1)} %collective-permute-done.mine_ref), channel_id=1, source_target_pairs={{0,1},{1,0},{2,3},{3,2},{4,5},{5,4},{6,7},{7,6},{8,9},{9,8},{10,11... | collective-permute-start | bytes 614408 | tf_op jit(solution)/shard_map/ppermute | solution.py:478
  12.2 6.4 %collective-permute-start.4 = (f32[72,256]{1,0:T(8,128)S(1)}, f32[72,256]{1,0:T(8,128)S(1)}, u32[]{:S(2)}, u32[]{:S(2)}) collective-permute-start(f32[72,256]{1,0:T(8,128)S(1)} %get-tuple-element.19), channel_id=1, source_target_pairs={{0,192},{64,0},{128,64},{192,128},{1,193},{65,1},{129,65},{193,129... | collective-permute-start | bytes 221192 | tf_op jit(solution)/shard_map/ppermute | solution.py:467
  18.6 1.6 %collective-permute-start.5 = (f32[72,256]{1,0:T(8,128)S(1)}, f32[72,256]{1,0:T(8,128)S(1)}, u32[]{:S(2)}, u32[]{:S(2)}) collective-permute-start(f32[72,256]{1,0:T(8,128)S(1)} %collective-permute-done.4.mine_ref), channel_id=1, source_target_pairs={{0,1},{1,0},{2,3},{3,2},{4,5},{5,4},{6,7},{7,6},{8,9},{9,8},{10,11... | collective-permute-start | bytes 221192 | tf_op jit(solution)/shard_map/ppermute | solution.py:477
  23.5 2.3 %copy-start = (f32[256,256]{1,0:T(8,128)S(1)}, f32[256,256]{1,0:T(8,128)}, u32[]{:S(2)}) copy-start(f32[256,256]{1,0:T(8,128)} %h_ref.3) | copy-start | bytes 786436
  23.5 2.3 %copy-start.1 = (f32[256,256]{1,0:T(8,128)S(1)}, f32[256,256]{1,0:T(8,128)}, u32[]{:S(2)}) copy-start(f32[256,256]{1,0:T(8,128)} %c_ref.3) | copy-start | bytes 786436

commit v6 on v5

--- a/solution.py
+++ b/solution.py
@@ -282,7 +282,7 @@
     )(e, eta, rounds, hamiltonian, coupling, g, near)
 
 
-def tables_body(near_ref, mode_ref, d_ref, near_out, mode_out, inverse_out, next_out, rounds_out, weight_out, wide):
+def tables_body(_, __, near_ref, mode_ref, d_ref, near_out, mode_out, inverse_out, next_out, rounds_out, weight_out, wide):
     wide[0, :, :NEIGH] = near_ref[...].T
     wide[1, :, :NEIGH] = mode_ref[...].T
     near_parts, mode_parts = (
@@ -330,7 +330,7 @@
         weight_out[:, 2 * total + m * size : 2 * total + (m + 1) * size] = low
 
 
-def tables(neighbors, phonon_modes, propagator):
+def tables(e, eta, neighbors, phonon_modes, propagator):
     modes_count, energies = propagator.shape[1:3]
     return pl.pallas_call(
         tables_body,
@@ -342,12 +342,12 @@
             jax.ShapeDtypeStruct((8, 128), F32),
             jax.ShapeDtypeStruct((2 * energies, 6 * modes_count * energies), BF16),
         ),
-        in_specs=[VMEM, VMEM, VMEM],
+        in_specs=[SMEM, SMEM, VMEM, VMEM, VMEM],
         out_specs=(VMEM, VMEM, VMEM, VMEM, VMEM, VMEM),
         scratch_shapes=[pltpu.VMEM((2, B, 128), jnp.int32)],
         compiler_params=PARAMS,
         name="tables",
-    )(neighbors, phonon_modes, propagator)
+    )(e, eta, neighbors, phonon_modes, propagator)
 
 
 def convolve_body(modes_count, weight_ref, mode_ref, green_ref, out_ref):
@@ -381,6 +381,8 @@
 ):
     pass_on = pltpu.make_async_copy(self_ref, self_out, sems.at[0])
     pass_on.start()
+    p_thirds = thirds(p_ref[0], p_ref[1])
+    square_real, square_imag = complex_product(p_thirds, p_thirds)
     part_real = self_ref[:, 0, :]
     part_imag = self_ref[:, 1, :]
 
@@ -426,8 +428,6 @@
                 moved[2 * part + side, pl.ds(q, ROWS, stride=GROUPS), :] = piece
     moved_real = jnp.concatenate([moved[0], moved[1]], axis=1)
     moved_imag = jnp.concatenate([moved[2], moved[3]], axis=1)
-    p_thirds = thirds(p_ref[0], p_ref[1])
-    square_real, square_imag = complex_product(p_thirds, p_thirds)
     right = thirds(square_real + moved_real, square_imag + moved_imag)
     left = thirds(g_real, g_imag)
     first = three_passes(left[0], right[0])
@@ -476,7 +476,9 @@
     far_other = lax.ppermute(far, "core", swap)
     head_other = lax.ppermute(head0, "core", swap)
     close_other = lax.ppermute(close, "core", swap)
-    near, mode, inverse, follower, rounds, weight = tables(neighbors.T, phonon_modes.T, propagator)
+    near, mode, inverse, follower, rounds, weight = tables(
+        energies, broadening, neighbors.T, phonon_modes.T, propagator
+    )
     rounds = jnp.max(rounds[:1]).astype(jnp.int32).reshape(1)
     g = first(energies, broadening, head0, head_other)
     g = middle(2, energies, broadening, far, far_other, g)

time: 66.5 us -> 66.6 us (level)
  no operation moved by 1% of the time
where the time goes in v6:
time: 66.6 us; the launch traced here: 66.4 us
  blocking collectives  35 us (53%)
  Pallas kernels  14.3 us (21%)
  starting transfers between devices  8.96 us (13%)
  waiting for transfers between devices  4.55 us (7%)
  between operations  2.92 us (4%)
    all_to_all x1, blocking collectives, body(): regrouped = lax.all_to_all(pairs, ENERGY, 0, 0, tiled=True)  21.4 us
    all_to_all x1, blocking collectives, body(): returned = lax.all_to_all(owned, ENERGY, 0, 0, tiled=True)  13.6 us
    ppermute x2, starting transfers between devices, shifted(): lax.ppermute(x, 'slab', [(i, (i + distance) % count) for i in range(count)])  5.57 us
    ppermute x1, waiting for transfers between devices, body(): far = lax.ppermute(piece, 'slab', [(0, 2), (1, 3), (2, 1), (3, 0)])  4.54 us
    pallas_call x2, Pallas kernels, middle(): pl.pallas_call(functools.partial(middle_body, distance), out_shape=G_SHAP...  4.33 us
    pallas_call x1, Pallas kernels, correct(): pl.pallas_call(correct_body, out_shape=(jax.ShapeDtypeStruct((1, 2, B, B)...  2.64 us
    pallas_call x1, Pallas kernels, last(): pl.pallas_call(last_body, out_shape=(G_SHAPE, G_SHAPE, jax.ShapeDtypeStru...  2.41 us
    pallas_call x1, Pallas kernels, tables(): pl.pallas_call(tables_body, out_shape=(jax.ShapeDtypeStruct((ROWS, 128),...  2.38 us
  transfers between devices with their start and end apart: 6, of which 1 were waited for; matrix products, arithmetic and copies ran while one was open for 1% of the time, Pallas kernels for 8%

profile of v6, /device:TPU:7, one launch (start us, length us, event | category | flops | bytes accessed | tf_op | source)
XLA Modules:
  0.0 66.4 jit_solution(12931292633261958633)
XLA Ops:
  0.6 0.0 copy-start.2
  0.6 0.0 copy-start.3
  0.7 0.0 copy-start.4
  0.7 1.1 %pack.1 = (f32[72,256]{1,0:T(8,128)S(1)}, f32[200,256]{1,0:T(8,128)S(1)}) custom-call(f32[256,256]{1,0:T(8,128)} %h_ref.3, f32[256,256]{1,0:T(8,128)} %c_ref.3), custom_call_target="tpu_custom_call" | custom-call | tf_op jit(solution)/shard_map/pack/pallas_call | solution.py:104
  1.7 0.1 collective-permute-start.2
  1.8 2.9 %collective-permute-start = (f32[200,256]{1,0:T(8,128)S(1)}, f32[200,256]{1,0:T(8,128)S(1)}, u32[]{:S(2)}, u32[]{:S(2)}) collective-permute-start(f32[200,256]{1,0:T(8,128)S(1)} %get-tuple-element.18), channel_id=1, source_target_pairs={{0,64},{64,128},{128,192},{192,0},{1,65},{65,129},{129,193},{193,1... | collective-permute-start | bytes 614408 | tf_op jit(solution)/shard_map/ppermute | solution.py:467
  4.8 4.5 %collective-permute-done.2.mine_ref = f32[200,256]{1,0:T(8,128)S(1)} collective-permute-done((f32[200,256]{1,0:T(8,128)S(1)}, f32[200,256]{1,0:T(8,128)S(1)}, u32[]{:S(2)}, u32[]{:S(2)}) %collective-permute-start.2) | collective-permute-done | bytes 204832 | tf_op jit(solution)/shard_map/ppermute | solution.py:473
  9.3 1.5 %collective-permute-start.3 = (f32[200,256]{1,0:T(8,128)S(1)}, f32[200,256]{1,0:T(8,128)S(1)}, u32[]{:S(2)}, u32[]{:S(2)}) collective-permute-start(f32[200,256]{1,0:T(8,128)S(1)} %collective-permute-done.2.mine_ref), channel_id=1, source_target_pairs={{0,1},{1,0},{2,3},{3,2},{4,5},{5,4},{6,7},{7,6},{8,9},{9,8},{10,11... | collective-permute-start | bytes 614408 | tf_op jit(solution)/shard_map/ppermute | solution.py:476
  10.8 0.0 collective-permute-done.mine_ref
  10.8 1.4 %collective-permute-start.1 = (f32[200,256]{1,0:T(8,128)S(1)}, f32[200,256]{1,0:T(8,128)S(1)}, u32[]{:S(2)}, u32[]{:S(2)}) collective-permute-start(f32[200,256]{1,0:T(8,128)S(1)} %collective-permute-done.mine_ref), channel_id=1, source_target_pairs={{0,1},{1,0},{2,3},{3,2},{4,5},{5,4},{6,7},{7,6},{8,9},{9,8},{10,11... | collective-permute-start | bytes 614408 | tf_op jit(solution)/shard_map/ppermute | solution.py:478
  12.2 2.6 %collective-permute-start.4 = (f32[72,256]{1,0:T(8,128)S(1)}, f32[72,256]{1,0:T(8,128)S(1)}, u32[]{:S(2)}, u32[]{:S(2)}) collective-permute-start(f32[72,256]{1,0:T(8,128)S(1)} %get-tuple-element.19), channel_id=1, source_target_pairs={{0,192},{64,0},{128,64},{192,128},{1,193},{65,1},{129,65},{193,129... | collective-permute-start | bytes 221192 | tf_op jit(solution)/shard_map/ppermute | solution.py:467
  16.2 0.0 copy-done.2
  16.2 0.0 copy-done.3
  16.2 0.0 copy-done.4
  16.2 2.4 %tables.1 = (s32[64,128]{1,0:T(8,128)S(1)}, s32[8,128]{1,0:T(8,128)S(1)}, s32[256,256]{1,0:T(8,128)S(1)}, s32[3,64,128]{2,1,0:T(8,128)S(1)}, f32[8,128]{1,0:T(8,128)S(1)}, /*index=5*/bf16[128,2304]{1,0:T(8,128)(2,1)S(1)}) custom-call(f32[1]{0:T(128)S(6)} %copy.9._.e_ref, f32[1]{0:T(128)S(6)} %copy.10.__.eta_ref, s32[32,256]{1,0:T(8,128)S(1)} %bitcast.6, ...), custom_call_target="tpu_custom_call" | custom-call | tf_op jit(solution)/shard_map/tables/pallas_call | solution.py:335
  18.6 0.0 collective-permute-done.4.mine_ref
  18.6 0.4 collective-permute-start.5
  19.0 0.6 slice_reduce_fusion
  20.2 0.0 collective-permute-done.5.other_ref
  20.3 1.1 %first.1.g_in = f32[2,256,256]{2,1,0:T(8,128)S(1)} custom-call(f32[1]{0:T(128)S(6)} %copy.9._.e_ref, f32[1]{0:T(128)S(6)} %copy.10.__.eta_ref, f32[72,256]{1,0:T(8,128)S(1)} %collective-permute-done.4.mine_ref, f32[72,256]{1,0:T(8,128)S(1)} %collective-permute-done.5.other_ref), custom_call_target="tpu_custom_call" | custom-call | tf_op jit(solution)/shard_map/first/pallas_call | solution.py:250
  21.4 0.0 collective-permute-done.3.other_ref
  21.4 2.1 %middle.2.g_in = f32[2,256,256]{2,1,0:T(8,128)S(1)} custom-call(f32[1]{0:T(128)S(6)} %copy.9._.e_ref, f32[1]{0:T(128)S(6)} %copy.10.__.eta_ref, f32[200,256]{1,0:T(8,128)S(1)} %collective-permute-done.2.mine_ref, f32[200,256]{1,0:T(8,128)S(1)} %collective-permute-done.3.other_ref, f32[2,256,256]{2,1,0:T(8,128)S(1)} %first.1.g_in), custom_call_target="tpu_custom_call" | custom-call | tf_op jit(solution)/shard_map/middle/pallas_call | solution.py:262
  23.5 0.0 copy-start
  23.5 0.0 copy-start.1
  23.5 0.0 collective-permute-done.1.other_ref
  23.5 2.3 %middle.3.g_in = f32[2,256,256]{2,1,0:T(8,128)S(1)} custom-call(f32[1]{0:T(128)S(6)} %copy.9._.e_ref, f32[1]{0:T(128)S(6)} %copy.10.__.eta_ref, f32[200,256]{1,0:T(8,128)S(1)} %collective-permute-done.mine_ref, f32[200,256]{1,0:T(8,128)S(1)} %collective-permute-done.1.other_ref, f32[2,256,256]{2,1,0:T(8,128)S(1)} %middle.2.g_in), custom_call_target="tpu_custom_call" | custom-call | tf_op jit(solution)/shard_map/middle/pallas_call | solution.py:262
  25.8 0.0 copy-done
  25.8 0.0 copy-done.1
  25.8 2.4 %last.1 = (f32[2,256,256]{2,1,0:T(8,128)S(1)}, f32[2,256,256]{2,1,0:T(8,128)S(1)}, f32[64,2,128]{2,1,0:T(2,128)S(1)}) custom-call(f32[1]{0:T(128)S(6)} %copy.9._.e_ref, f32[1]{0:T(128)S(6)} %copy.10.__.eta_ref, s32[1]{0:T(128)} %bitcast.2._.rounds_ref, f32[256,256]{1,0:T(8,128)S(1)} %copy-done, f32[256,256]{1,0:T(8,128)S(1)} %copy-done.1, ...), custom_call_target="tpu_custom_call" | custom-call | tf_op jit(solution)/shard_map/last/pallas_call | solution.py:274
  28.2 21.4 %all_to_all.10.green_ref = f32[64,2,128]{2,1,0:T(2,128)S(1)} all-to-all(f32[64,2,128]{2,1,0:T(2,128)S(1)} %get-tuple-element.21), channel_id=1, replica_groups=mesh['slab'=4,'y'=4,'z'=8,'core'=2] {'y','z','core'}, dimensions={0} | all-to-all | bytes 131072 | tf_op jit(solution)/shard_map/all_to_all | solution.py:487
  49.6 0.3 convolve.1
  50.0 13.6 %all_to_all.11.self_ref = f32[64,2,128]{2,1,0:T(2,128)S(1)} all-to-all(f32[64,2,128]{2,1,0:T(2,128)S(1)} %convolve.1), channel_id=1, replica_groups=mesh['slab'=4,'y'=4,'z'=8,'core'=2] {'y','z','core'}, dimensions={0} | all-to-all | bytes 131072 | tf_op jit(solution)/shard_map/all_to_all | solution.py:489
  63.6 2.6 %correct.1 = (f32[1,2,256,256]{3,2,1,0:T(8,128)}, f32[64,2,128]{2,1,0:T(2,128)}) custom-call(s32[1]{0:T(128)} %bitcast.2._.rounds_ref, f32[64,2,128]{2,1,0:T(2,128)S(1)} %all_to_all.11.self_ref, s32[3,64,128]{2,1,0:T(8,128)S(1)} %get-tuple-element.22.next_ref, s32[256,256]{1,0:T(8,128)S(1)} %get-tuple-element.23.inverse_ref, ...), custom_call_target="tpu_custom_call" | custom-call | tf_op jit(solution)/shard_map/correct/pallas_call | solution.py:447
Async XLA Ops:
  0.6 15.6 %copy-start.2 = (f32[2,6,64,64]{3,2,1,0:T(8,128)S(1)}, f32[2,6,64,64]{3,2,1,0:T(8,128)}, u32[]{:S(2)}) copy-start(f32[2,6,64,64]{3,2,1,0:T(8,128)} %d_ref.1) | copy-start | bytes 589828
  0.6 15.6 %copy-start.3 = (s32[256,32]{0,1:T(8,128)S(1)}, s32[256,32]{0,1:T(8,128)}, u32[]{:S(2)}) copy-start(s32[256,32]{0,1:T(8,128)} %param.12) | copy-start | bytes 98308
  0.7 15.6 %copy-start.4 = (s32[256,32]{0,1:T(8,128)S(1)}, s32[256,32]{0,1:T(8,128)}, u32[]{:S(2)}) copy-start(s32[256,32]{0,1:T(8,128)} %param.13) | copy-start | bytes 98308
  1.7 7.6 %collective-permute-start.2 = (f32[200,256]{1,0:T(8,128)S(1)}, f32[200,256]{1,0:T(8,128)S(1)}, u32[]{:S(2)}, u32[]{:S(2)}) collective-permute-start(f32[200,256]{1,0:T(8,128)S(1)} %get-tuple-element.18), channel_id=1, source_target_pairs={{0,128},{64,192},{128,64},{192,0},{1,129},{65,193},{129,65},{193,1... | collective-permute-start | bytes 614408 | tf_op jit(solution)/shard_map/ppermute | solution.py:473
  1.8 9.0 %collective-permute-start = (f32[200,256]{1,0:T(8,128)S(1)}, f32[200,256]{1,0:T(8,128)S(1)}, u32[]{:S(2)}, u32[]{:S(2)}) collective-permute-start(f32[200,256]{1,0:T(8,128)S(1)} %get-tuple-element.18), channel_id=1, source_target_pairs={{0,64},{64,128},{128,192},{192,0},{1,65},{65,129},{129,193},{193,1... | collective-permute-start | bytes 614408 | tf_op jit(solution)/shard_map/ppermute | solution.py:467
  9.3 12.1 %collective-permute-start.3 = (f32[200,256]{1,0:T(8,128)S(1)}, f32[200,256]{1,0:T(8,128)S(1)}, u32[]{:S(2)}, u32[]{:S(2)}) collective-permute-start(f32[200,256]{1,0:T(8,128)S(1)} %collective-permute-done.2.mine_ref), channel_id=1, source_target_pairs={{0,1},{1,0},{2,3},{3,2},{4,5},{5,4},{6,7},{7,6},{8,9},{9,8},{10,11... | collective-permute-start | bytes 614408 | tf_op jit(solution)/shard_map/ppermute | solution.py:476
  10.8 12.7 %collective-permute-start.1 = (f32[200,256]{1,0:T(8,128)S(1)}, f32[200,256]{1,0:T(8,128)S(1)}, u32[]{:S(2)}, u32[]{:S(2)}) collective-permute-start(f32[200,256]{1,0:T(8,128)S(1)} %collective-permute-done.mine_ref), channel_id=1, source_target_pairs={{0,1},{1,0},{2,3},{3,2},{4,5},{5,4},{6,7},{7,6},{8,9},{9,8},{10,11... | collective-permute-start | bytes 614408 | tf_op jit(solution)/shard_map/ppermute | solution.py:478
  12.2 6.4 %collective-permute-start.4 = (f32[72,256]{1,0:T(8,128)S(1)}, f32[72,256]{1,0:T(8,128)S(1)}, u32[]{:S(2)}, u32[]{:S(2)}) collective-permute-start(f32[72,256]{1,0:T(8,128)S(1)} %get-tuple-element.19), channel_id=1, source_target_pairs={{0,192},{64,0},{128,64},{192,128},{1,193},{65,1},{129,65},{193,129... | collective-permute-start | bytes 221192 | tf_op jit(solution)/shard_map/ppermute | solution.py:467
  18.6 1.6 %collective-permute-start.5 = (f32[72,256]{1,0:T(8,128)S(1)}, f32[72,256]{1,0:T(8,128)S(1)}, u32[]{:S(2)}, u32[]{:S(2)}) collective-permute-start(f32[72,256]{1,0:T(8,128)S(1)} %collective-permute-done.4.mine_ref), channel_id=1, source_target_pairs={{0,1},{1,0},{2,3},{3,2},{4,5},{5,4},{6,7},{7,6},{8,9},{9,8},{10,11... | collective-permute-start | bytes 221192 | tf_op jit(solution)/shard_map/ppermute | solution.py:477
  23.5 2.3 %copy-start = (f32[256,256]{1,0:T(8,128)S(1)}, f32[256,256]{1,0:T(8,128)}, u32[]{:S(2)}) copy-start(f32[256,256]{1,0:T(8,128)} %h_ref.3) | copy-start | bytes 786436
  23.5 2.3 %copy-start.1 = (f32[256,256]{1,0:T(8,128)S(1)}, f32[256,256]{1,0:T(8,128)}, u32[]{:S(2)}) copy-start(f32[256,256]{1,0:T(8,128)} %c_ref.3) | copy-start | bytes 786436
